TPU v7x, 512 devices: a whole 4x4x16 slice. The times are simulated.
512 devices in a mesh: leaf: 32 (over x, y, core), blk: 16 (over z).
Axes of the slice: x: 4, y: 4, z: 16, core: 2. Of those that a mesh axis runs over, the one named last changes fastest.
Arguments:
- points: float32 [3, 131072], P(None, ('leaf', 'blk')), may hold values from 0 to 1
- iterate: bfloat16 [131072, 256], P(('leaf', 'blk')), may hold values from -6 to 6
- right_side: float32 [131072, 256], P(('leaf', 'blk')), may hold values from -6 to 6
- near_mask: int32 [512, 16], P(('leaf', 'blk')), may hold values from 0 to 1, as said below
- leaf_inverse: bfloat16 [512, 256, 256], P(('leaf', 'blk'))
- skeleton: int32 [3, 32, 512], P(None, 'leaf'), may hold values from 0 to 4095, as said below
- coupling: bfloat16 [3, 32, 512, 512], P(None, 'leaf'), may hold values from -0.25 to 0.25
- reduced_inverse: bfloat16 [3, 32, 512, 512], P(None, 'leaf')
- lift: bfloat16 [3, 131072, 512], P(None, ('leaf', 'blk')), may hold values from -0.25 to 0.25
Outputs:
- correction: float32 [131072, 256], P(('leaf', 'blk'))
Inputs may be any that keep to these rules, and one draw needn't show every extreme that they name: near_mask[i, i mod 16] is 1. `skeleton`: the 512 indices of one level and subtree are distinct.
All inputs are finite; a program needn't handle non-finite values.
Results may differ from a plain program's by a relative error of at most 0.014.
Values may be sent and summed in bfloat16 or wider, within the bound.
No kernel may reach another device: no remote copies, remote signals or barrier semaphores. Data moves between devices by JAX's collectives and lax.ppermute only.
A program may use at most 64 MiB of HBM per device.

v0:
```python
import jax
import jax.numpy as jnp
from jax import lax
from jax.sharding import PartitionSpec as P

LEVELS = 3


kernel_scale = 0.125
spread_coef = 4.0
shift_value = 1.0


def from_partner(block, axis, distance):
    count = lax.axis_size(axis)
    route = []
    for low in range(count):
        high = low | 1 << distance
        if high != low and high < count:
            route += [(low, high), (high, low)]
    return lax.ppermute(block, axis, route)


def kernel_block(left, right):
    dist = jnp.zeros((left.shape[1], right.shape[1]), jnp.float32)
    for axis_no in range(3):
        diff = left[axis_no][:, None] - right[axis_no][None, :]
        dist = dist + diff * diff
    return kernel_scale * jnp.exp(-spread_coef * dist)


def sibling_solve(cpl, inverse, part_total, level_no):
    own_total = part_total
    for bit_no in range(level_no):
        own_total = own_total + from_partner(own_total, "leaf", bit_no)
    other_total = from_partner(own_total.astype(jnp.bfloat16), "leaf", level_no).astype(
        own_total.dtype
    )
    rhs = own_total - jnp.dot(
        cpl, other_total.astype(jnp.bfloat16), preferred_element_type=jnp.float32
    )
    return jnp.dot(inverse, rhs.astype(jnp.bfloat16), preferred_element_type=jnp.float32)


def on_device(
    points, iterate, right_side, near_mask, leaf_inverse, skeleton, coupling, reduced_inverse, lift
):
    tile_rows = points.shape[1]
    all_pts = lax.all_gather(points, "blk", axis=1, tiled=True)
    mask_row = near_mask[0].astype(jnp.bfloat16)
    block_rows = lax.all_gather(iterate, "blk", axis=0, tiled=True)
    count = block_rows.shape[0]
    col_block = jnp.arange(count, dtype=jnp.int32) // tile_rows
    col_mask = jnp.take(mask_row, col_block)
    kernel = kernel_block(points, all_pts).astype(jnp.bfloat16)
    near = jnp.dot(kernel * col_mask[None, :], block_rows, preferred_element_type=jnp.float32)
    resid = right_side - shift_value * iterate.astype(jnp.float32) - near
    field = jnp.dot(leaf_inverse[0], resid.astype(jnp.bfloat16), preferred_element_type=jnp.float32)
    blk_start = lax.axis_index("blk") * tile_rows
    for level_no in range(LEVELS):
        local_index = skeleton[level_no, 0] - blk_start
        inside = (local_index >= 0) & (local_index < tile_rows)
        rows_taken = jnp.take(field, jnp.clip(local_index, 0, tile_rows - 1), axis=0)
        picked = jnp.where(inside[:, None], rows_taken, 0.0)
        part_total = lax.psum(picked, "blk")
        answer = sibling_solve(
            coupling[level_no, 0], reduced_inverse[level_no, 0], part_total, level_no
        ).astype(jnp.bfloat16)
        field = field - jnp.dot(lift[level_no], answer, preferred_element_type=jnp.float32)
    return field


def solution(mesh):
    in_specs = (
        P(None, ("leaf", "blk")),
        P(("leaf", "blk"), None),
        P(("leaf", "blk"), None),
        P(("leaf", "blk"), None),
        P(("leaf", "blk"), None, None),
        P(None, "leaf", None),
        P(None, "leaf", None, None),
        P(None, "leaf", None, None),
        P(None, ("leaf", "blk"), None),
    )
    out_specs = P(("leaf", "blk"), None)
    return jax.shard_map(
        on_device, mesh=mesh, in_specs=in_specs, out_specs=out_specs, check_vma=False
    )
```

profile of v0, /device:TPU:6, one launch (start us, length us, event | category | flops | bytes accessed | tf_op | source)
XLA Modules:
  0.0 568.9 jit_solution(15477949225896639626)
XLA Ops:
  8.5 36.0 %all_gather.6 = f32[3,4096]{1,0:T(4,128)S(1)} all-gather(f32[3,256]{1,0:T(4,128)} %param.11), channel_id=1, replica_groups=mesh['leaf'=32,'blk'=16] {'blk'}, dimensions={1}, use_global_device_ids=true | all-gather | bytes 52224 | tf_op jit(solution)/shard_map/all_gather | solution.py:49
  45.2 4.3 fusion.67
  51.8 5.7 %fusion.69 = bf16[4096]{0:T(1024)(128)(2,1)S(1)} fusion(pred[4096]{0:T(1024)(128)(4,1)S(1)} %compare_reduce_fusion, pred[4096]{0:T(1024)(128)(4,1)S(1)} %compare_reduce_fusion.1, pred[4096]{0:T(1024)(128)(4,1)S(1)} %compare_reduce_fusion.2, pred[4096]{0:T(1024)(128)(4,1)S(1)} %compare_reduce_fusion.3, pred[4096]{0:T(1024)(128)(4,1)S(1)} %compare_reduce_fusion.4, ...), kind=kLoop, calls=%fused_computation.94 | loop fusion | flops 98304 | bytes 53266 | tf_op jit(solution)/shard_map/jit(_take)/select_n | solution.py:54
  57.6 29.1 %all-gather.2.cloned.1.call-done = bf16[4096,256]{1,0:T(8,128)(2,1)} async-done(((bf16[256,256]{1,0:T(8,128)(2,1)}), bf16[4096,256]{1,0:T(8,128)(2,1)}) %all-gather.2.cloned.1.call-update) | async-done | bytes 2097168 | tf_op jit(solution)/shard_map/all_gather | solution.py:51
  86.7 3.9 convolution_bitcast_fusion.3
  90.8 1.6 gather_fusion
  93.5 134.9 %all-reduce.4.cloned.1.call-done = f32[512,256]{1,0:T(8,128)} async-done(((f32[512,256]{1,0:T(8,128)}), f32[512,256]{1,0:T(8,128)}) %all-reduce.4.cloned.1.call-update) | async-done | bytes 524304 | tf_op jit(solution)/shard_map/psum | solution.py:65
  229.4 1.9 collective-permute-start
  234.2 1.6 fusion.25
  235.9 1.6 gather_fusion.1
  238.6 134.5 %all-reduce.6.cloned.1.call-done = f32[512,256]{1,0:T(8,128)} async-done(((f32[512,256]{1,0:T(8,128)}), f32[512,256]{1,0:T(8,128)}) %all-reduce.6.cloned.1.call-update) | async-done | bytes 524304 | tf_op jit(solution)/shard_map/psum | solution.py:65
  373.1 1.9 collective-permute-start.1
  375.0 2.1 collective-permute-done.1
  378.2 3.4 collective-permute-start.2
  381.7 6.8 %collective-permute-done.2 = bf16[512,256]{1,0:T(8,128)(2,1)S(1)} collective-permute-done((bf16[512,256]{1,0:T(8,128)(2,1)S(1)}, bf16[512,256]{1,0:T(8,128)(2,1)S(1)}, u32[]{:S(2)}, u32[]{:S(2)}) %collective-permute-start.2) | collective-permute-done | bytes 262176 | tf_op jit(solution)/shard_map/ppermute | solution.py:21
  388.8 1.6 fusion.24
  390.5 1.6 gather_fusion.2
  393.1 134.6 %all-reduce.8.cloned.1.call-done = f32[512,256]{1,0:T(8,128)} async-done(((f32[512,256]{1,0:T(8,128)}), f32[512,256]{1,0:T(8,128)}) %all-reduce.8.cloned.1.call-update) | async-done | bytes 524304 | tf_op jit(solution)/shard_map/psum | solution.py:65
  527.7 1.9 collective-permute-start.3
  529.6 2.1 collective-permute-done.3
  532.8 3.4 collective-permute-start.4
  536.2 12.5 %collective-permute-done.4 = f32[512,256]{1,0:T(8,128)S(1)} collective-permute-done((f32[512,256]{1,0:T(8,128)S(1)}, f32[512,256]{1,0:T(8,128)S(1)}, u32[]{:S(2)}, u32[]{:S(2)}) %collective-permute-start.4) | collective-permute-done | bytes 524320 | tf_op jit(solution)/shard_map/ppermute | solution.py:21
  548.8 4.9 collective-permute-start.5
  553.7 6.0 %collective-permute-done.5 = bf16[512,256]{1,0:T(8,128)(2,1)S(1)} collective-permute-done((bf16[512,256]{1,0:T(8,128)(2,1)S(1)}, bf16[512,256]{1,0:T(8,128)(2,1)S(1)}, u32[]{:S(2)}, u32[]{:S(2)}) %collective-permute-start.5) | collective-permute-done | bytes 262176 | tf_op jit(solution)/shard_map/ppermute | solution.py:21
  (54 shorter events, 17.7 us)
Async XLA Ops:
  6.5 80.1 %copy-start = (bf16[1,256,256]{2,1,0:T(8,128)(2,1)S(1)}, bf16[1,256,256]{2,1,0:T(8,128)(2,1)}, u32[]{:S(2)}) copy-start(bf16[1,256,256]{2,1,0:T(8,128)(2,1)} %param.15) | copy-start | bytes 393220
  6.5 80.1 %all-gather.2.cloned.1.call-start = ((), (), s32[]{:S(2)}) async-start(), calls=%async_computation | async-start | bytes 2228224 | tf_op jit(solution)/shard_map/all_gather | solution.py:51
  7.3 221.1 %all-reduce.4.cloned.1.call-start = ((), (), s32[]{:S(2)}) async-start(), calls=%async_computation.1 | async-start | bytes 1048576 | tf_op jit(solution)/shard_map/psum | solution.py:65
  92.3 140.5 %copy-start.1 = (bf16[3,1,512,512]{3,2,1,0:T(8,128)(2,1)S(1)}, bf16[3,1,512,512]{3,2,1,0:T(8,128)(2,1)}, u32[]{:S(2)}) copy-start(bf16[3,1,512,512]{3,2,1,0:T(8,128)(2,1)} %param.17) | copy-start | bytes 4718596
  93.4 279.7 %all-reduce.6.cloned.1.call-start = ((), (), s32[]{:S(2)}) async-start(), calls=%async_computation.2 | async-start | bytes 1048576 | tf_op jit(solution)/shard_map/psum | solution.py:65
  229.4 3.4 collective-permute-start
  238.5 150.3 %copy-start.2 = (bf16[3,256,512]{2,1,0:T(8,128)(2,1)S(1)}, bf16[3,256,512]{2,1,0:T(8,128)(2,1)}, u32[]{:S(2)}) copy-start(bf16[3,256,512]{2,1,0:T(8,128)(2,1)} %param.19) | copy-start | bytes 2359300
  238.5 289.2 %all-reduce.8.cloned.1.call-start = ((), (), s32[]{:S(2)}) async-start(), calls=%async_computation.3 | async-start | bytes 1048576 | tf_op jit(solution)/shard_map/psum | solution.py:65
  373.1 4.0 collective-permute-start.1
  378.2 10.2 %collective-permute-start.2 = (bf16[512,256]{1,0:T(8,128)(2,1)S(1)}, bf16[512,256]{1,0:T(8,128)(2,1)S(1)}, u32[]{:S(2)}, u32[]{:S(2)}) collective-permute-start(bf16[512,256]{1,0:T(8,128)(2,1)S(1)} %get-tuple-element.11), channel_id=1, source_target_pairs={{0,32},{32,0},{16,48},{48,16},{64,96},{96,64},{80,112},{112,80},{1... | collective-permute-start | bytes 786440 | tf_op jit(solution)/shard_map/ppermute | solution.py:21
  527.7 4.0 collective-permute-start.3
  532.8 15.9 %collective-permute-start.4 = (f32[512,256]{1,0:T(8,128)S(1)}, f32[512,256]{1,0:T(8,128)S(1)}, u32[]{:S(2)}, u32[]{:S(2)}) collective-permute-start(f32[512,256]{1,0:T(8,128)S(1)} %add.73), channel_id=1, source_target_pairs={{0,32},{32,0},{16,48},{48,16},{64,96},{96,64},{80,112},{112,80},{1... | collective-permute-start | bytes 1572872 | tf_op jit(solution)/shard_map/ppermute | solution.py:21
  548.8 10.9 %collective-permute-start.5 = (bf16[512,256]{1,0:T(8,128)(2,1)S(1)}, bf16[512,256]{1,0:T(8,128)(2,1)S(1)}, u32[]{:S(2)}, u32[]{:S(2)}) collective-permute-start(bf16[512,256]{1,0:T(8,128)(2,1)S(1)} %get-tuple-element.9), channel_id=1, source_target_pairs={{0,64},{64,0},{16,80},{80,16},{32,96},{96,32},{48,112},{112,48},{1... | collective-permute-start | bytes 786440 | tf_op jit(solution)/shard_map/ppermute | solution.py:21
Sparse Core Ops, SparseCore 0:
  9.4 77.2 all-gather.1
  93.5 134.7 all-reduce.3
  238.7 134.3 all-reduce.5
  393.2 134.4 all-reduce.7
where the time goes:
time: 570 us; the launch traced here: 569 us
  waiting for transfers between devices  465 us (82%)
  blocking collectives  36 us (6%)
  other arithmetic  19.1 us (3%)
  starting transfers between devices  17.6 us (3%)
  between operations  13.4 us (2%)
  matrix products  10.6 us (2%)
  local copies, waits for them, and re-layouts  7.5 us (1%)
    psum x3, waiting for transfers between devices, on_device(): part_total = lax.psum(picked, 'blk')  404 us
    all_gather x1, blocking collectives, on_device(): all_pts = lax.all_gather(points, 'blk', axis=1, tiled=True)  36 us
    ppermute x6, waiting for transfers between devices, from_partner(): return lax.ppermute(block, axis, route)  30.9 us
    all_gather x1, waiting for transfers between devices, on_device(): block_rows = lax.all_gather(iterate, 'blk', axis=0, tiled=True)  29.1 us
    ppermute x6, starting transfers between devices, from_partner(): return lax.ppermute(block, axis, route)  17.5 us
  transfers between devices with their start and end apart: 10, of which 10 were waited for; matrix products, arithmetic and copies ran while one was open for 3% of the time, Pallas kernels for 0%

commit v1 on v0

v1 whole, which is shorter than its diff:
```python
import math

import jax
import jax.numpy as jnp
from jax import lax
from jax.experimental import pallas as pl
from jax.experimental.pallas import tpu as pltpu
from jax.sharding import PartitionSpec as P

LEVELS = 3
CELL = 4

kernel_scale = 0.125
spread_coef = 4.0
shift_value = 1.0

EXTRA = 8
OFF_BIAS = 30000.0
EXP2_COEF = spread_coef * math.log2(math.e)
EXP2_BASE = math.log2(kernel_scale)

F32 = jnp.float32
BF16 = jnp.bfloat16
VMEM = pl.BlockSpec(memory_space=pltpu.VMEM)
SMEM = pl.BlockSpec(memory_space=pltpu.SMEM)


def dot_nt(left, right):
    return lax.dot_general(left, right, (((1,), (1,)), ((), ())), preferred_element_type=F32)


def dot_tn(left, right):
    return lax.dot_general(left, right, (((0,), (0,)), ((), ())), preferred_element_type=F32)


def dot_nn(left, right):
    return jnp.dot(left, right, preferred_element_type=F32)


def split_parts(value):
    high = value.astype(BF16).astype(F32)
    rest = value - high
    mid = rest.astype(BF16).astype(F32)
    return high, mid, (rest - mid).astype(BF16).astype(F32)


def pack_kernel(points_ref, iterate_ref, mask_ref, out_ref, extra_ref):
    count, rows, pts = out_ref.shape
    block = rows - EXTRA
    point = points_ref[...]
    high = point.astype(BF16).astype(F32)
    extra_ref[...] = jnp.zeros_like(extra_ref)
    extra_ref[0:3, :] = high
    extra_ref[3:4, 0 : mask_ref.shape[1]] = mask_ref[...].astype(F32)
    extra_ref[4:7, :] = point - high
    turned = iterate_ref[...].astype(F32).T.astype(BF16)
    extra = extra_ref[...].astype(BF16)
    for dest in range(count):
        part = dest % CELL
        out_ref[dest, 0:block, :] = turned[part * block : (part + 1) * block]
        out_ref[dest, block:rows, :] = extra


def near_kernel(cell_ref, recv_ref, out_ref, acc_ref):
    count, rows, pts = recv_ref.shape
    block = rows - EXTRA
    first = cell_ref[0]
    row_no = lax.broadcasted_iota(jnp.int32, (EXTRA, pts), 0)
    lane_no = lax.broadcasted_iota(jnp.int32, (EXTRA, pts), 1)
    coord_rows = (row_no % 4) != 3
    three_rows = row_no < 3

    def coords(extra):
        whole = jnp.where(coord_rows, extra + pltpu.roll(extra, 4, 0), 0.0)
        square = jnp.sum(jnp.where(three_rows, whole * whole, 0.0), axis=0, keepdims=True)
        return whole, square

    def rows_of(parts):
        high, mid, low = parts
        picked = jnp.where(row_no == 1, mid, low)
        return jnp.where(three_rows, jnp.where(row_no == 0, high, picked), 0.0)

    left = []
    masks = []
    for member in range(CELL):
        extra = recv_ref[first + member, block:rows, :].astype(F32)
        masks.append(extra[3:4, :])
        whole, square = coords(extra)
        parts = split_parts(2.0 * EXP2_COEF * whole)
        own = split_parts(EXP2_BASE - EXP2_COEF * square)
        unit = jnp.where(three_rows | (row_no == 3 + member), 1.0, 0.0)
        left.append(jnp.concatenate([*parts, rows_of(own), unit], axis=0))
    left = jnp.concatenate(left, axis=1).astype(BF16)
    ones = jnp.where(three_rows, 1.0, 0.0)
    acc_ref[...] = jnp.zeros_like(acc_ref)

    def step(tile, carry):
        extra = recv_ref[tile, block:rows, :].astype(F32)
        whole, square = coords(extra)
        tail = rows_of(split_parts(-EXP2_COEF * square))
        for member in range(CELL):
            chosen = jnp.where(lane_no[0:1] == tile, masks[member], 0.0)
            flag = jnp.sum(chosen, axis=1, keepdims=True)
            tail = jnp.where(row_no == 3 + member, (flag - 1.0) * OFF_BIAS, tail)
        right = jnp.concatenate([extra, extra, extra, ones, tail], axis=0).astype(BF16)
        value = jnp.exp2(dot_tn(right, left)).astype(BF16)
        acc_ref[...] += dot_nn(recv_ref[tile, 0:block, :], value)
        return carry

    lax.fori_loop(0, count, step, 0)
    for member in range(CELL):
        out_ref[member] = acc_ref[:, member * pts : (member + 1) * pts].astype(BF16)


def send_field(field, out_ref):
    turned = field.T.astype(BF16)
    out_ref[...] = turned.reshape(out_ref.shape)


def leaf_kernel(near_ref, right_ref, iterate_ref, inverse_ref, field_ref, out_ref):
    parts, block, pts = near_ref.shape
    near = near_ref[...].reshape(parts * block, pts).astype(F32).T
    resid = right_ref[...] - shift_value * iterate_ref[...].astype(F32) - near
    field = dot_nn(inverse_ref[0], resid.astype(BF16))
    field_ref[...] = field
    send_field(field, out_ref)


def pick_kernel(level_no, recv_ref, skeleton_ref, out_ref):
    tiles, cols, pts = recv_ref.shape
    index = skeleton_ref[level_no]
    count = index.shape[1]
    tile_of = index // pts
    inner = index - tile_of * pts
    row_no = lax.broadcasted_iota(jnp.int32, (pts, count), 0)
    chosen = jnp.where(row_no == inner, 1.0, 0.0).astype(BF16)
    lanes = dot_nn(recv_ref[...].reshape(tiles * cols, pts), chosen)
    total = jnp.zeros((cols, count), F32)
    for tile in range(tiles):
        total = total + jnp.where(tile_of == tile, lanes[tile * cols : (tile + 1) * cols], 0.0)
    total = total.astype(BF16)
    if len(out_ref.shape) == 2:
        out_ref[...] = total
    else:
        for copy in range(out_ref.shape[0]):
            out_ref[copy] = total


def solve_kernel(level_no, leaf_ref, nodes_ref, coupling_ref, inverse_ref, out_ref):
    half = nodes_ref.shape[0] // 2
    low = nodes_ref[0].astype(F32)
    high = nodes_ref[half].astype(F32)
    for member in range(1, half):
        low = low + nodes_ref[member].astype(F32)
        high = high + nodes_ref[half + member].astype(F32)
    upper = ((leaf_ref[0] >> level_no) & 1) == 1
    own = jnp.where(upper, high, low)
    other = jnp.where(upper, low, high)
    rhs = own - dot_nt(other.astype(BF16), coupling_ref[0, 0])
    answer = dot_nt(rhs.astype(BF16), inverse_ref[0, 0]).astype(BF16)
    for copy in range(out_ref.shape[0]):
        out_ref[copy] = answer


def lift_kernel(field_ref, lift_ref, answer_ref, *out_refs):
    tiles, cols, count = answer_ref.shape
    answer = answer_ref[...].reshape(tiles * cols, count)
    field = field_ref[...] - dot_nt(lift_ref[0], answer)
    out_refs[0][...] = field
    if len(out_refs) > 1:
        send_field(field, out_refs[1])


def level_spec(shape, level_no):
    tail = (0,) * (len(shape) - 1)
    return pl.BlockSpec((1,) + tuple(shape[1:]), lambda step: (level_no,) + tail)


def whole_spec(shape):
    zeros = (0,) * len(shape)
    return pl.BlockSpec(tuple(shape), lambda step: zeros)


def on_device(
    points, iterate, right_side, near_mask, leaf_inverse, skeleton, coupling, reduced_inverse, lift
):
    blk_count = lax.axis_size("blk")
    leaf_count = lax.axis_size("leaf")
    pts, cols = iterate.shape
    slots = skeleton.shape[2]
    share = cols // blk_count
    block = cols // CELL
    leaf_no = lax.axis_index("leaf").astype(jnp.int32).reshape(1)
    first = (lax.axis_index("blk") // CELL * CELL).astype(jnp.int32).reshape(1)
    cells = [list(range(c, c + CELL)) for c in range(0, blk_count, CELL)]

    packed = pl.pallas_call(
        pack_kernel,
        out_shape=jax.ShapeDtypeStruct((blk_count, block + EXTRA, pts), BF16),
        in_specs=[VMEM] * 3,
        out_specs=VMEM,
        scratch_shapes=[pltpu.VMEM((EXTRA, pts), F32)],
        name="pack",
    )(points, iterate, near_mask)
    packed = lax.all_to_all(packed, "blk", 0, 0)
    near = pl.pallas_call(
        near_kernel,
        out_shape=jax.ShapeDtypeStruct((CELL, block, pts), BF16),
        in_specs=[SMEM, VMEM],
        out_specs=VMEM,
        scratch_shapes=[pltpu.VMEM((block, CELL * pts), F32)],
        name="near",
    )(first, packed)
    near = lax.all_to_all(near, "blk", 0, 0, axis_index_groups=cells)
    field_shape = jax.ShapeDtypeStruct((pts, cols), F32)
    send_shape = jax.ShapeDtypeStruct((blk_count, share, pts), BF16)
    field, sent = pl.pallas_call(
        leaf_kernel,
        out_shape=(field_shape, send_shape),
        in_specs=[VMEM] * 4,
        out_specs=(VMEM, VMEM),
        name="leaf",
    )(near, right_side, iterate, leaf_inverse)

    for level_no in range(LEVELS):
        width = 2 << level_no
        groups = [list(range(c, c + width)) for c in range(0, leaf_count, width)]
        spread = level_no == 2
        sent = lax.all_to_all(sent, "blk", 0, 0)
        node_shape = (width, share, slots)
        nodes = pl.pallas_call(
            lambda *refs, level_no=level_no: pick_kernel(level_no, *refs),
            out_shape=jax.ShapeDtypeStruct(node_shape if spread else node_shape[1:], BF16),
            in_specs=[VMEM] * 2,
            out_specs=VMEM,
            name="pick",
        )(sent, skeleton)
        if spread:
            nodes = lax.all_to_all(nodes, "leaf", 0, 0, axis_index_groups=groups)
        else:
            nodes = lax.all_gather(nodes, "leaf", axis=0, axis_index_groups=groups)
        answer_shape = (blk_count, share, slots)
        answer = pl.pallas_call(
            lambda *refs, level_no=level_no: solve_kernel(level_no, *refs),
            out_shape=jax.ShapeDtypeStruct(answer_shape, BF16),
            grid=(1,),
            in_specs=[
                SMEM,
                whole_spec(node_shape),
                level_spec(coupling.shape, level_no),
                level_spec(reduced_inverse.shape, level_no),
            ],
            out_specs=whole_spec(answer_shape),
            name="solve",
        )(leaf_no, nodes, coupling, reduced_inverse)
        answer = lax.all_to_all(answer, "blk", 0, 0)
        last = level_no == LEVELS - 1
        results = pl.pallas_call(
            lift_kernel,
            out_shape=(field_shape,) if last else (field_shape, send_shape),
            grid=(1,),
            in_specs=[
                whole_spec(field.shape),
                level_spec(lift.shape, level_no),
                whole_spec(answer_shape),
            ],
            out_specs=tuple(
                whole_spec(s.shape) for s in ((field_shape,) if last else (field_shape, send_shape))
            ),
            name="lift",
        )(field, lift, answer)
        field = results[0]
        sent = None if last else results[1]
    return field


def solution(mesh):
    in_specs = (
        P(None, ("leaf", "blk")),
        P(("leaf", "blk"), None),
        P(("leaf", "blk"), None),
        P(("leaf", "blk"), None),
        P(("leaf", "blk"), None, None),
        P(None, "leaf", None),
        P(None, "leaf", None, None),
        P(None, "leaf", None, None),
        P(None, ("leaf", "blk"), None),
    )
    out_specs = P(("leaf", "blk"), None)
    return jax.shard_map(
        on_device, mesh=mesh, in_specs=in_specs, out_specs=out_specs, check_vma=False
    )
```

time: 570 us -> 244 us (0.43)
  waiting for transfers between devices: 465 us -> 44.2 us
  blocking collectives: 36 us -> 142 us
  Pallas kernels: 0 us -> 33.4 us
  other arithmetic: 19.1 us -> 0 us
  between operations: 13.4 us -> 0.05 us
  matrix products: 10.6 us -> 0 us
  local copies, waits for them, and re-layouts: 7.5 us -> 1.47 us
    psum x3 -> x0, waiting for transfers between devices: 404 us -> none  [on_device(): part_total = lax.psum(picked, 'blk')]
    all_to_all x0 -> x7, blocking collectives: none -> 132 us  [the longest x3 69 us: on_device(): answer = lax.all_to_all(answer, 'blk', 0, 0)]
    all_to_all x0 -> x2, waiting for transfers between devices: none -> 44.2 us  [the longest x1 30.8 us: on_device(): packed = lax.all_to_all(packed, 'blk', 0, 0)]
    pallas_call x0 -> x12, Pallas kernels: none -> 33.4 us  [the longest x1 10.7 us: on_device(): pl.pallas_call(near_kernel, out_shape=jax.ShapeDtypeStruct((CELL, block,...]
    ppermute x6 -> x0, waiting for transfers between devices: 30.9 us -> none  [from_partner(): return lax.ppermute(block, axis, route)]
    all_gather x1 -> x0, waiting for transfers between devices: 29.1 us -> none  [on_device(): block_rows = lax.all_gather(iterate, 'blk', axis=0, tiled=True)]
    all_gather x1 -> x2, blocking collectives: 36 us -> 9.87 us  [on_device(): nodes = lax.all_gather(nodes, 'leaf', axis=0, axis_index_groups=groups)]
    all_to_all x0 -> x2, starting transfers between devices: none -> 21.5 us  [the longest x1 15.2 us: on_device(): packed = lax.all_to_all(packed, 'blk', 0, 0)]
  transfers between devices with their start and end apart: 10 -> 2, of which waited for: 10 -> 2; matrix products, arithmetic and copies ran while one was open for 3% -> 0% of each run, Pallas kernels for 0% -> 0%
where the time goes in v1:
time: 244 us; the launch traced here: 243 us
  blocking collectives  142 us (58%)
  waiting for transfers between devices  44.2 us (18%)
  Pallas kernels  33.4 us (14%)
  starting transfers between devices  21.5 us (9%)
    all_to_all x3, blocking collectives, on_device(): answer = lax.all_to_all(answer, 'blk', 0, 0)  69 us
    all_to_all x2, blocking collectives, on_device(): sent = lax.all_to_all(sent, 'blk', 0, 0)  41.2 us
    all_to_all x1, waiting for transfers between devices, on_device(): packed = lax.all_to_all(packed, 'blk', 0, 0)  30.8 us
    all_to_all x1, starting transfers between devices, on_device(): packed = lax.all_to_all(packed, 'blk', 0, 0)  15.2 us
    all_to_all x1, waiting for transfers between devices, on_device(): sent = lax.all_to_all(sent, 'blk', 0, 0)  13.4 us
    all_to_all x1, blocking collectives, on_device(): near = lax.all_to_all(near, 'blk', 0, 0, axis_index_groups=cells)  11.4 us
    pallas_call x1, Pallas kernels, on_device(): pl.pallas_call(near_kernel, out_shape=jax.ShapeDtypeStruct((CELL, block,...  10.7 us
    all_to_all x1, blocking collectives, on_device(): nodes = lax.all_to_all(nodes, 'leaf', 0, 0, axis_index_groups=groups)  10.4 us
  transfers between devices with their start and end apart: 2, of which 2 were waited for; matrix products, arithmetic and copies ran while one was open for 0% of the time, Pallas kernels for 0%

profile of v1, /device:TPU:6, one launch (start us, length us, event | category | flops | bytes accessed | tf_op | source)
XLA Modules:
  0.0 242.5 jit_solution(15877354561566812033)
XLA Ops:
  0.0 1.8 pack.1
  1.8 15.2 %all-to-all-start = ((bf16[16,72,256]{2,1,0:T(8,128)(2,1)}), bf16[16,72,256]{2,1,0:T(8,128)(2,1)S(1)}, u32[]{:S(2)}, u32[]{:S(2)}) async-start(bf16[16,72,256]{2,1,0:T(8,128)(2,1)} %pack.1), calls=%async_computation | async-start | bytes 1179648 | tf_op jit(solution)/shard_map/all_to_all | solution.py:205
  17.1 30.8 %all-to-all-done.recv_ref = bf16[16,72,256]{2,1,0:T(8,128)(2,1)S(1)} async-done(((bf16[16,72,256]{2,1,0:T(8,128)(2,1)}), bf16[16,72,256]{2,1,0:T(8,128)(2,1)S(1)}, u32[]{:S(2)}, u32[]{:S(2)}) %all-to-all-start) | async-done | bytes 589856 | tf_op jit(solution)/shard_map/all_to_all | solution.py:205
  48.7 10.7 %near.1 = bf16[4,64,256]{2,1,0:T(8,128)(2,1)} custom-call(s32[1]{0:T(128)} %bitcast.cell_ref, bf16[16,72,256]{2,1,0:T(8,128)(2,1)} %copy-done), custom_call_target="tpu_custom_call" | custom-call | tf_op jit(solution)/shard_map/near/pallas_call | solution.py:206
  59.4 11.4 %all_to_all.45.near_ref = bf16[4,64,256]{2,1,0:T(8,128)(2,1)} all-to-all(bf16[4,64,256]{2,1,0:T(8,128)(2,1)} %near.1), channel_id=1, replica_groups={{0,1,2,3},{4,5,6,7},{8,9,10,11},{12,13,14,15},{16,17,18,19},{20,21,22,2..., dimensions={0} | all-to-all | bytes 262144 | tf_op jit(solution)/shard_map/all_to_all | solution.py:214
  70.8 2.1 leaf.1
  72.9 6.3 %all-to-all-start.2 = ((bf16[16,16,256]{2,1,0:T(8,128)(2,1)}), bf16[16,16,256]{2,1,0:T(8,128)(2,1)S(1)}, u32[]{:S(2)}, u32[]{:S(2)}) async-start(bf16[16,16,256]{2,1,0:T(8,128)(2,1)} %get-tuple-element.12), calls=%async_computation.2 | async-start | bytes 262144 | tf_op jit(solution)/shard_map/all_to_all | solution.py:229
  79.2 13.4 %all-to-all-done.2.refs_0_ = bf16[16,16,256]{2,1,0:T(8,128)(2,1)S(1)} async-done(((bf16[16,16,256]{2,1,0:T(8,128)(2,1)}), bf16[16,16,256]{2,1,0:T(8,128)(2,1)S(1)}, u32[]{:S(2)}, u32[]{:S(2)}) %all-to-all-start.2) | async-done | bytes 131104 | tf_op jit(solution)/shard_map/all_to_all | solution.py:229
  95.1 3.1 %all-gather = bf16[32,512]{1,0:T(8,128)(2,1)} all-gather(bf16[16,512]{1,0:T(8,128)(2,1)} %pick.3), channel_id=2, replica_groups={{0,16},{32,48},{64,80},{96,112},{128,144},{160,176},{192,208},{224,240}..., dimensions={0}, use_global_device_ids=true | all-gather | bytes 49152 | tf_op jit(solution)/shard_map/all_gather | solution.py:241
  98.2 2.4 solve.3
  100.6 23.2 %all_to_all.46.answer_ref = bf16[16,16,512]{2,1,0:T(8,128)(2,1)} all-to-all(bf16[16,16,512]{2,1,0:T(8,128)(2,1)} %solve.3), channel_id=1, replica_groups=mesh['leaf'=32,'blk'=16] {'blk'}, dimensions={0} | all-to-all | bytes 524288 | tf_op jit(solution)/shard_map/all_to_all | solution.py:256
  123.7 2.1 lift.3
  125.9 20.6 %all_to_all.47.refs_0_ = bf16[16,16,256]{2,1,0:T(8,128)(2,1)} all-to-all(bf16[16,16,256]{2,1,0:T(8,128)(2,1)} %get-tuple-element.14), channel_id=1, replica_groups=mesh['leaf'=32,'blk'=16] {'blk'}, dimensions={0} | all-to-all | bytes 262144 | tf_op jit(solution)/shard_map/all_to_all | solution.py:229
  146.4 1.8 pick.4
  148.2 6.7 %all-gather.1 = bf16[64,512]{1,0:T(8,128)(2,1)} all-gather(bf16[16,512]{1,0:T(8,128)(2,1)} %pick.4), channel_id=3, replica_groups={{0,16,32,48},{64,80,96,112},{128,144,160,176},{192,208,224,240},{256,27..., dimensions={0}, use_global_device_ids=true | all-gather | bytes 81920 | tf_op jit(solution)/shard_map/all_gather | solution.py:241
  154.9 2.4 solve.4
  157.3 23.2 %all_to_all.48.answer_ref = bf16[16,16,512]{2,1,0:T(8,128)(2,1)} all-to-all(bf16[16,16,512]{2,1,0:T(8,128)(2,1)} %solve.4), channel_id=1, replica_groups=mesh['leaf'=32,'blk'=16] {'blk'}, dimensions={0} | all-to-all | bytes 524288 | tf_op jit(solution)/shard_map/all_to_all | solution.py:256
  180.5 2.1 lift.4
  182.6 20.6 %all_to_all.49.refs_0_ = bf16[16,16,256]{2,1,0:T(8,128)(2,1)} all-to-all(bf16[16,16,256]{2,1,0:T(8,128)(2,1)} %get-tuple-element.16), channel_id=1, replica_groups=mesh['leaf'=32,'blk'=16] {'blk'}, dimensions={0} | all-to-all | bytes 262144 | tf_op jit(solution)/shard_map/all_to_all | solution.py:229
  203.2 1.8 pick.5
  205.0 10.4 %all_to_all.50.refs_1_ = bf16[8,16,512]{2,1,0:T(8,128)(2,1)} all-to-all(bf16[8,16,512]{2,1,0:T(8,128)(2,1)} %pick.5), channel_id=1, replica_groups={{0,16,32,48,64,80,96,112},{128,144,160,176,192,208,224,240},{256,272,28..., dimensions={0} | all-to-all | bytes 262144 | tf_op jit(solution)/shard_map/all_to_all | solution.py:239
  215.4 2.4 solve.5
  217.8 22.6 %all_to_all.51.answer_ref = bf16[16,16,512]{2,1,0:T(8,128)(2,1)} all-to-all(bf16[16,16,512]{2,1,0:T(8,128)(2,1)} %solve.5), channel_id=1, replica_groups=mesh['leaf'=32,'blk'=16] {'blk'}, dimensions={0} | all-to-all | bytes 524288 | tf_op jit(solution)/shard_map/all_to_all | solution.py:256
  240.4 2.1 lift.5
  (5 shorter events, 3.2 us)
Async XLA Ops:
  1.8 46.0 %all-to-all-start = ((bf16[16,72,256]{2,1,0:T(8,128)(2,1)}), bf16[16,72,256]{2,1,0:T(8,128)(2,1)S(1)}, u32[]{:S(2)}, u32[]{:S(2)}) async-start(bf16[16,72,256]{2,1,0:T(8,128)(2,1)} %pack.1), calls=%async_computation | async-start | bytes 1179648 | tf_op jit(solution)/shard_map/all_to_all | solution.py:205
  47.9 0.8 copy-start
  72.9 19.8 %all-to-all-start.2 = ((bf16[16,16,256]{2,1,0:T(8,128)(2,1)}), bf16[16,16,256]{2,1,0:T(8,128)(2,1)S(1)}, u32[]{:S(2)}, u32[]{:S(2)}) async-start(bf16[16,16,256]{2,1,0:T(8,128)(2,1)} %get-tuple-element.12), calls=%async_computation.2 | async-start | bytes 262144 | tf_op jit(solution)/shard_map/all_to_all | solution.py:229
  92.7 0.7 copy-start.1

commit v2 on v1

--- a/solution.py
+++ b/solution.py
@@ -126,27 +126,46 @@
     send_field(field, out_ref)
 
 
-def pick_kernel(level_no, recv_ref, skeleton_ref, out_ref):
-    tiles, cols, pts = recv_ref.shape
-    index = skeleton_ref[level_no]
+def pick_rows(field, index):
+    tiles, cols, pts = field.shape
     count = index.shape[1]
     tile_of = index // pts
     inner = index - tile_of * pts
     row_no = lax.broadcasted_iota(jnp.int32, (pts, count), 0)
     chosen = jnp.where(row_no == inner, 1.0, 0.0).astype(BF16)
-    lanes = dot_nn(recv_ref[...].reshape(tiles * cols, pts), chosen)
+    lanes = dot_nn(field.reshape(tiles * cols, pts), chosen)
     total = jnp.zeros((cols, count), F32)
     for tile in range(tiles):
         total = total + jnp.where(tile_of == tile, lanes[tile * cols : (tile + 1) * cols], 0.0)
-    total = total.astype(BF16)
+    return total.astype(BF16)
+
+
+def store_copies(value, out_ref):
     if len(out_ref.shape) == 2:
-        out_ref[...] = total
+        out_ref[...] = value
     else:
         for copy in range(out_ref.shape[0]):
-            out_ref[copy] = total
-
-
-def solve_kernel(level_no, leaf_ref, nodes_ref, coupling_ref, inverse_ref, out_ref):
+            out_ref[copy] = value
+
+
+def pick_kernel(recv_ref, skeleton_ref, out_ref):
+    store_copies(pick_rows(recv_ref[...], skeleton_ref[0]), out_ref)
+
+
+def update_kernel(level_no, field_ref, answer_ref, lift_ref, skeleton_ref, next_ref, out_ref):
+    step = pl.program_id(0)
+    answer = answer_ref[...]
+    tiles = lift_ref.shape[0]
+    for tile in range(tiles):
+        spot = step * tiles + tile
+        next_ref[spot] = field_ref[spot].astype(F32) - dot_nt(answer, lift_ref[tile])
+
+    @pl.when(step == pl.num_programs(0) - 1)
+    def _():
+        store_copies(pick_rows(next_ref[...].astype(BF16), skeleton_ref[level_no + 1]), out_ref)
+
+
+def solve_kernel(level_no, leaf_ref, nodes_ref, coupling_ref, inverse_ref, *refs):
     half = nodes_ref.shape[0] // 2
     low = nodes_ref[0].astype(F32)
     high = nodes_ref[half].astype(F32)
@@ -158,17 +177,21 @@
     other = jnp.where(upper, low, high)
     rhs = own - dot_nt(other.astype(BF16), coupling_ref[0, 0])
     answer = dot_nt(rhs.astype(BF16), inverse_ref[0, 0]).astype(BF16)
-    for copy in range(out_ref.shape[0]):
-        out_ref[copy] = answer
-
-
-def lift_kernel(field_ref, lift_ref, answer_ref, *out_refs):
-    tiles, cols, count = answer_ref.shape
-    answer = answer_ref[...].reshape(tiles * cols, count)
-    field = field_ref[...] - dot_nt(lift_ref[0], answer)
-    out_refs[0][...] = field
-    if len(out_refs) > 1:
-        send_field(field, out_refs[1])
+    share = answer.shape[0]
+    earlier, out_ref = refs[:-1], refs[-1]
+    for spot, value_ref in enumerate(earlier):
+        out_ref[spot * share : (spot + 1) * share] = value_ref[...]
+    out_ref[len(earlier) * share : (len(earlier) + 1) * share] = answer
+
+
+def lift_kernel(field_ref, lift_ref, answer_ref, out_ref):
+    blocks, rows, count = answer_ref.shape
+    share = rows // LEVELS
+    field = field_ref[...]
+    for level_no in range(LEVELS):
+        answer = answer_ref[:, level_no * share : (level_no + 1) * share, :]
+        field = field - dot_nt(lift_ref[level_no], answer.reshape(blocks * share, count))
+    out_ref[...] = field
 
 
 def level_spec(shape, level_no):
@@ -194,6 +217,7 @@
     first = (lax.axis_index("blk") // CELL * CELL).astype(jnp.int32).reshape(1)
     cells = [list(range(c, c + CELL)) for c in range(0, blk_count, CELL)]
 
+    lifts = [lax.all_gather(lift[level_no], "blk", axis=0) for level_no in range(LEVELS - 1)]
     packed = pl.pallas_call(
         pack_kernel,
         out_shape=jax.ShapeDtypeStruct((blk_count, block + EXTRA, pts), BF16),
@@ -222,24 +246,44 @@
         name="leaf",
     )(near, right_side, iterate, leaf_inverse)
 
+    sent = lax.all_to_all(sent, "blk", 0, 0)
+    answers = []
     for level_no in range(LEVELS):
+        last = level_no == LEVELS - 1
         width = 2 << level_no
         groups = [list(range(c, c + width)) for c in range(0, leaf_count, width)]
         spread = level_no == 2
-        sent = lax.all_to_all(sent, "blk", 0, 0)
         node_shape = (width, share, slots)
-        nodes = pl.pallas_call(
-            lambda *refs, level_no=level_no: pick_kernel(level_no, *refs),
-            out_shape=jax.ShapeDtypeStruct(node_shape if spread else node_shape[1:], BF16),
-            in_specs=[VMEM] * 2,
-            out_specs=VMEM,
-            name="pick",
-        )(sent, skeleton)
+        pick_shape = jax.ShapeDtypeStruct(node_shape if spread else node_shape[1:], BF16)
+        if level_no == 0:
+            nodes = pl.pallas_call(
+                pick_kernel,
+                out_shape=pick_shape,
+                in_specs=[VMEM] * 2,
+                out_specs=VMEM,
+                name="pick",
+            )(sent, skeleton)
+        else:
+            kept_shape = jax.ShapeDtypeStruct(sent.shape, F32)
+            sent, nodes = pl.pallas_call(
+                lambda *refs, level_no=level_no - 1: update_kernel(level_no, *refs),
+                out_shape=(kept_shape, pick_shape),
+                grid=(blk_count // CELL,),
+                in_specs=[
+                    whole_spec(sent.shape),
+                    whole_spec((share, slots)),
+                    pl.BlockSpec((CELL, pts, slots), lambda step: (step, 0, 0)),
+                    whole_spec(skeleton.shape),
+                ],
+                out_specs=(whole_spec(kept_shape.shape), whole_spec(pick_shape.shape)),
+                name="update",
+            )(sent, answers[-1], lifts[level_no - 1], skeleton)
         if spread:
             nodes = lax.all_to_all(nodes, "leaf", 0, 0, axis_index_groups=groups)
         else:
             nodes = lax.all_gather(nodes, "leaf", axis=0, axis_index_groups=groups)
-        answer_shape = (blk_count, share, slots)
+        earlier = answers if last else []
+        answer_shape = ((len(earlier) + 1) * share, slots)
         answer = pl.pallas_call(
             lambda *refs, level_no=level_no: solve_kernel(level_no, *refs),
             out_shape=jax.ShapeDtypeStruct(answer_shape, BF16),
@@ -249,29 +293,20 @@
                 whole_spec(node_shape),
                 level_spec(coupling.shape, level_no),
                 level_spec(reduced_inverse.shape, level_no),
-            ],
+            ]
+            + [whole_spec((share, slots))] * len(earlier),
             out_specs=whole_spec(answer_shape),
             name="solve",
-        )(leaf_no, nodes, coupling, reduced_inverse)
-        answer = lax.all_to_all(answer, "blk", 0, 0)
-        last = level_no == LEVELS - 1
-        results = pl.pallas_call(
-            lift_kernel,
-            out_shape=(field_shape,) if last else (field_shape, send_shape),
-            grid=(1,),
-            in_specs=[
-                whole_spec(field.shape),
-                level_spec(lift.shape, level_no),
-                whole_spec(answer_shape),
-            ],
-            out_specs=tuple(
-                whole_spec(s.shape) for s in ((field_shape,) if last else (field_shape, send_shape))
-            ),
-            name="lift",
-        )(field, lift, answer)
-        field = results[0]
-        sent = None if last else results[1]
-    return field
+        )(leaf_no, nodes, coupling, reduced_inverse, *earlier)
+        answers.append(answer)
+    answer = lax.all_gather(answers[-1], "blk", axis=0)
+    return pl.pallas_call(
+        lift_kernel,
+        out_shape=field_shape,
+        in_specs=[VMEM] * 3,
+        out_specs=VMEM,
+        name="lift",
+    )(field, lift, answer)
 
 
 def solution(mesh):

time: 244 us -> 258 us (1.057)
  blocking collectives: 142 us -> 66.5 us
  waiting for transfers between devices: 44.2 us -> 114 us
  between operations: 0.05 us -> 13.4 us
  starting transfers between devices: 21.5 us -> 24.6 us
    all_to_all x5 -> x0, blocking collectives: 110 us -> none  [the longest x3 69 us: on_device(): answer = lax.all_to_all(answer, 'blk', 0, 0)]
    all_gather x0 -> x2, waiting for transfers between devices: none -> 61 us  [on_device(): lax.all_gather(lift[level_no], 'blk', axis=0)]
    all_gather x0 -> x1, blocking collectives: none -> 35.7 us  [on_device(): answer = lax.all_gather(answers[-1], 'blk', axis=0)]
    all_to_all x1, waiting for transfers between devices: 30.8 us -> 36.6 us  [on_device(): packed = lax.all_to_all(packed, 'blk', 0, 0)]
    all_to_all x1, starting transfers between devices: 6.32 us -> 9.36 us  [on_device(): sent = lax.all_to_all(sent, 'blk', 0, 0)]
    pallas_call x6 -> x4, Pallas kernels: 11.6 us -> 13.7 us  [the longest x2 9.41 us: on_device(): pl.pallas_call(lambda *refs, level_no=level_no - 1: update_kernel(level_n...]
  transfers between devices with their start and end apart: 2 -> 4, of which waited for: 2 -> 3; matrix products, arithmetic and copies ran while one was open for 0% -> 0% of each run, Pallas kernels for 0% -> 10%
where the time goes in v2:
time: 258 us; the launch traced here: 257 us
  waiting for transfers between devices  114 us (44%)
  blocking collectives  66.5 us (26%)
  Pallas kernels  35.3 us (14%)
  starting transfers between devices  24.6 us (10%)
  between operations  13.4 us (5%)
  local copies, waits for them, and re-layouts  3.39 us (1%)
    all_gather x2, waiting for transfers between devices, on_device(): lax.all_gather(lift[level_no], 'blk', axis=0)  61 us
    all_to_all x1, waiting for transfers between devices, on_device(): packed = lax.all_to_all(packed, 'blk', 0, 0)  36.6 us
    all_gather x1, blocking collectives, on_device(): answer = lax.all_gather(answers[-1], 'blk', axis=0)  35.7 us
    all_to_all x1, waiting for transfers between devices, on_device(): sent = lax.all_to_all(sent, 'blk', 0, 0)  15.5 us
    all_to_all x1, starting transfers between devices, on_device(): packed = lax.all_to_all(packed, 'blk', 0, 0)  15.2 us
    pallas_call x1, Pallas kernels, on_device(): pl.pallas_call(near_kernel, out_shape=jax.ShapeDtypeStruct((CELL, block,...  10.7 us
    all_to_all x1, blocking collectives, on_device(): nodes = lax.all_to_all(nodes, 'leaf', 0, 0, axis_index_groups=groups)  10.6 us
    all_to_all x1, blocking collectives, on_device(): near = lax.all_to_all(near, 'blk', 0, 0, axis_index_groups=cells)  10.5 us
  transfers between devices with their start and end apart: 4, of which 3 were waited for; matrix products, arithmetic and copies ran while one was open for 0% of the time, Pallas kernels for 10%

profile of v2, /device:TPU:6, one launch (start us, length us, event | category | flops | bytes accessed | tf_op | source)
XLA Modules:
  0.0 257.1 jit_solution(1719111524195979498)
XLA Ops:
  6.5 1.9 fusion
  8.5 0.7 all-gather.8.cloned.1.call-update
  9.2 1.9 pack.1
  11.1 15.2 %all-to-all-start = ((bf16[16,72,256]{2,1,0:T(8,128)(2,1)}), bf16[16,72,256]{2,1,0:T(8,128)(2,1)S(1)}, u32[]{:S(2)}, u32[]{:S(2)}) async-start(bf16[16,72,256]{2,1,0:T(8,128)(2,1)} %pack.1), calls=%async_computation | async-start | bytes 1179648 | tf_op jit(solution)/shard_map/all_to_all | solution.py:229
  26.3 36.6 %all-to-all-done.recv_ref = bf16[16,72,256]{2,1,0:T(8,128)(2,1)S(1)} async-done(((bf16[16,72,256]{2,1,0:T(8,128)(2,1)}), bf16[16,72,256]{2,1,0:T(8,128)(2,1)S(1)}, u32[]{:S(2)}, u32[]{:S(2)}) %all-to-all-start) | async-done | bytes 589856 | tf_op jit(solution)/shard_map/all_to_all | solution.py:229
  62.9 0.9 copy-done
  63.7 10.7 %near.1 = bf16[4,64,256]{2,1,0:T(8,128)(2,1)} custom-call(s32[1]{0:T(128)} %bitcast.cell_ref, bf16[16,72,256]{2,1,0:T(8,128)(2,1)} %copy-done), custom_call_target="tpu_custom_call" | custom-call | tf_op jit(solution)/shard_map/near/pallas_call | solution.py:230
  74.5 10.5 %all_to_all.20.near_ref = bf16[4,64,256]{2,1,0:T(8,128)(2,1)} all-to-all(bf16[4,64,256]{2,1,0:T(8,128)(2,1)} %near.1), channel_id=1, replica_groups={{0,1,2,3},{4,5,6,7},{8,9,10,11},{12,13,14,15},{16,17,18,19},{20,21,22,2..., dimensions={0} | all-to-all | bytes 262144 | tf_op jit(solution)/shard_map/all_to_all | solution.py:238
  84.9 2.2 leaf.1
  87.1 9.4 %all-to-all-start.2 = ((bf16[16,16,256]{2,1,0:T(8,128)(2,1)}), bf16[16,16,256]{2,1,0:T(8,128)(2,1)S(1)}, u32[]{:S(2)}, u32[]{:S(2)}) async-start(bf16[16,16,256]{2,1,0:T(8,128)(2,1)} %get-tuple-element.11), calls=%async_computation.2 | async-start | bytes 262144 | tf_op jit(solution)/shard_map/all_to_all | solution.py:249
  96.5 15.5 %all-to-all-done.2.recv_ref.refs_0_ = bf16[16,16,256]{2,1,0:T(8,128)(2,1)S(1)} async-done(((bf16[16,16,256]{2,1,0:T(8,128)(2,1)}), bf16[16,16,256]{2,1,0:T(8,128)(2,1)S(1)}, u32[]{:S(2)}, u32[]{:S(2)}) %all-to-all-start.2) | async-done | bytes 131104 | tf_op jit(solution)/shard_map/all_to_all | solution.py:249
  112.0 0.7 copy-done.1
  112.6 1.8 pick.1
  114.4 3.1 %all-gather = bf16[32,512]{1,0:T(8,128)(2,1)} all-gather(bf16[16,512]{1,0:T(8,128)(2,1)} %pick.1), channel_id=2, replica_groups={{0,16},{32,48},{64,80},{96,112},{128,144},{160,176},{192,208},{224,240}..., dimensions={0}, use_global_device_ids=true | all-gather | bytes 49152 | tf_op jit(solution)/shard_map/all_gather | solution.py:284
  117.5 2.2 solve.3.refs_1_.refs_4_
  119.7 4.7 %update.2 = (f32[16,16,256]{2,1,0:T(8,128)}, bf16[16,512]{1,0:T(8,128)(2,1)}) custom-call(bf16[16,16,256]{2,1,0:T(8,128)(2,1)} %copy-done.1, bf16[16,512]{1,0:T(8,128)(2,1)} %solve.3.refs_1_.refs_4_, bf16[16,256,512]{2,1,0:T(8,128)(2,1)} %all-gather.6.cloned.1.call-done.refs_2_, s32[3,1,512]{2,1,0:T(1,128)} %refs_3_.8), custom_call_target="tpu_custom_call" | custom-call | tf_op jit(solution)/shard_map/update/pallas_call | solution.py:268
  124.4 6.6 %all-gather.1 = bf16[64,512]{1,0:T(8,128)(2,1)} all-gather(bf16[16,512]{1,0:T(8,128)(2,1)} %get-tuple-element.13), channel_id=3, replica_groups={{0,16,32,48},{64,80,96,112},{128,144,160,176},{192,208,224,240},{256,27..., dimensions={0}, use_global_device_ids=true | all-gather | bytes 81920 | tf_op jit(solution)/shard_map/all_gather | solution.py:284
  131.0 2.2 solve.4.refs_1_.refs_5_
  133.3 61.0 %all-gather.8.cloned.1.call-done.refs_2_ = bf16[16,256,512]{2,1,0:T(8,128)(2,1)} async-done(((bf16[1,256,512]{2,1,0:T(8,128)(2,1)}), bf16[16,256,512]{2,1,0:T(8,128)(2,1)}) %all-gather.8.cloned.1.call-update) | async-done | bytes 4194320 | tf_op jit(solution)/shard_map/all_gather | solution.py:220
  194.3 4.7 %update.3 = (f32[16,16,256]{2,1,0:T(8,128)}, bf16[8,16,512]{2,1,0:T(8,128)(2,1)}) custom-call(f32[16,16,256]{2,1,0:T(8,128)} %get-tuple-element.12.refs_0_, bf16[16,512]{1,0:T(8,128)(2,1)} %solve.4.refs_1_.refs_5_, bf16[16,256,512]{2,1,0:T(8,128)(2,1)} %all-gather.8.cloned.1.call-done.refs_2_, s32[3,1,512]{2,1,0:T(1,128)} %refs_3_.8), custom_call_target="tpu_custom_call" | custom-call | tf_op jit(solution)/shard_map/update/pallas_call | solution.py:268
  199.0 10.6 %all_to_all.21.refs_1_ = bf16[8,16,512]{2,1,0:T(8,128)(2,1)} all-to-all(bf16[8,16,512]{2,1,0:T(8,128)(2,1)} %get-tuple-element.14), channel_id=1, replica_groups={{0,16,32,48,64,80,96,112},{128,144,160,176,192,208,224,240},{256,272,28..., dimensions={0} | all-to-all | bytes 262144 | tf_op jit(solution)/shard_map/all_to_all | solution.py:282
  209.6 2.3 solve.5
  211.9 35.7 %all-gather.2 = bf16[768,512]{1,0:T(8,128)(2,1)} all-gather(bf16[48,512]{1,0:T(8,128)(2,1)} %solve.5), channel_id=4, replica_groups=mesh['leaf'=32,'blk'=16] {'blk'}, dimensions={0}, use_global_device_ids=true | all-gather | bytes 835584 | tf_op jit(solution)/shard_map/all_gather | solution.py:302
  247.7 2.6 lift.1
  (6 shorter events, 0.1 us)
Async XLA Ops:
  6.5 113.2 %all-gather.6.cloned.1.call-start = ((), (), s32[]{:S(2)}) async-start(), calls=%async_computation.4 | async-start | bytes 4456448 | tf_op jit(solution)/shard_map/all_gather | solution.py:220
  8.4 185.9 %all-gather.8.cloned.1.call-start = ((), (), s32[]{:S(2)}) async-start(), calls=%async_computation.5 | async-start | bytes 4456448 | tf_op jit(solution)/shard_map/all_gather | solution.py:220
  11.1 51.8 %all-to-all-start = ((bf16[16,72,256]{2,1,0:T(8,128)(2,1)}), bf16[16,72,256]{2,1,0:T(8,128)(2,1)S(1)}, u32[]{:S(2)}, u32[]{:S(2)}) async-start(bf16[16,72,256]{2,1,0:T(8,128)(2,1)} %pack.1), calls=%async_computation | async-start | bytes 1179648 | tf_op jit(solution)/shard_map/all_to_all | solution.py:229
  62.9 0.9 copy-start
  87.1 24.9 %all-to-all-start.2 = ((bf16[16,16,256]{2,1,0:T(8,128)(2,1)}), bf16[16,16,256]{2,1,0:T(8,128)(2,1)S(1)}, u32[]{:S(2)}, u32[]{:S(2)}) async-start(bf16[16,16,256]{2,1,0:T(8,128)(2,1)} %get-tuple-element.11), calls=%async_computation.2 | async-start | bytes 262144 | tf_op jit(solution)/shard_map/all_to_all | solution.py:249
  112.0 0.7 copy-start.1
Sparse Core Ops, SparseCore 0:
  9.4 107.5 all-gather.5
  119.0 75.2 all-gather.7

commit v3 on v2

--- a/solution.py
+++ b/solution.py
@@ -9,6 +9,7 @@
 
 LEVELS = 3
 CELL = 4
+ROOM = 64
 
 kernel_scale = 0.125
 spread_coef = 4.0
@@ -126,18 +127,20 @@
     send_field(field, out_ref)
 
 
+def equal_rows(count, value, kind):
+    row_no = lax.broadcasted_iota(jnp.int32, (count, value.shape[1]), 0)
+    return jnp.where(row_no == value, 1.0, 0.0).astype(kind)
+
+
 def pick_rows(field, index):
     tiles, cols, pts = field.shape
-    count = index.shape[1]
     tile_of = index // pts
-    inner = index - tile_of * pts
-    row_no = lax.broadcasted_iota(jnp.int32, (pts, count), 0)
-    chosen = jnp.where(row_no == inner, 1.0, 0.0).astype(BF16)
+    chosen = equal_rows(pts, index - tile_of * pts, BF16)
     lanes = dot_nn(field.reshape(tiles * cols, pts), chosen)
-    total = jnp.zeros((cols, count), F32)
+    total = jnp.zeros((cols, index.shape[1]), F32)
     for tile in range(tiles):
         total = total + jnp.where(tile_of == tile, lanes[tile * cols : (tile + 1) * cols], 0.0)
-    return total.astype(BF16)
+    return total
 
 
 def store_copies(value, out_ref):
@@ -148,21 +151,72 @@
             out_ref[copy] = value
 
 
-def pick_kernel(recv_ref, skeleton_ref, out_ref):
-    store_copies(pick_rows(recv_ref[...], skeleton_ref[0]), out_ref)
-
-
-def update_kernel(level_no, field_ref, answer_ref, lift_ref, skeleton_ref, next_ref, out_ref):
-    step = pl.program_id(0)
-    answer = answer_ref[...]
-    tiles = lift_ref.shape[0]
-    for tile in range(tiles):
-        spot = step * tiles + tile
-        next_ref[spot] = field_ref[spot].astype(F32) - dot_nt(answer, lift_ref[tile])
-
-    @pl.when(step == pl.num_programs(0) - 1)
-    def _():
-        store_copies(pick_rows(next_ref[...].astype(BF16), skeleton_ref[level_no + 1]), out_ref)
+def pick_kernel(recv_ref, skeleton_ref, *out_refs):
+    for level_no in range(LEVELS):
+        out_refs[level_no][...] = pick_rows(recv_ref[...], skeleton_ref[level_no]).astype(BF16)
+
+
+def plan_kernel(tiles, tile_ref, skeleton_ref, lift_ref, rows_ref, slot_ref, over_ref):
+    pts = lift_ref.shape[1]
+    row_no = lax.broadcasted_iota(jnp.int32, (pts, pts), 0)
+    lane_no = lax.broadcasted_iota(jnp.int32, (pts, pts), 1)
+    before = jnp.where(row_no < lane_no, 1.0, 0.0).astype(BF16)
+    own = lax.broadcasted_iota(jnp.int32, (tiles, pts), 0) == tile_ref[0]
+    room_no = lax.broadcasted_iota(jnp.int32, (ROOM, pts), 0).astype(F32)
+    most = jnp.zeros((tiles, pts), F32)
+    spot = 0
+    for level_no in range(1, LEVELS):
+        index = skeleton_ref[level_no]
+        tile_of = index // pts
+        inner = equal_rows(pts, index - tile_of * pts, BF16)
+        member = equal_rows(tiles, tile_of, F32)
+        present = dot_nt(member.astype(BF16), inner)
+        rank = dot_nn(present.astype(BF16), before)
+        ranks = jnp.sum(member * dot_nn(rank.astype(BF16), inner), axis=0, keepdims=True)
+        slot_ref[level_no - 1] = tile_of * ROOM + ranks.astype(jnp.int32)
+        most = jnp.maximum(most, rank + present)
+        own_present = jnp.sum(jnp.where(own, present, 0.0), axis=0, keepdims=True)
+        own_rank = jnp.sum(jnp.where(own, rank, 0.0), axis=0, keepdims=True)
+        chosen = jnp.where((room_no == own_rank) & (own_present > 0.5), 1.0, 0.0).astype(BF16)
+        for earlier in range(level_no):
+            rows_ref[spot * ROOM : (spot + 1) * ROOM] = dot_nn(chosen, lift_ref[earlier]).astype(BF16)
+            spot += 1
+    over_ref[0] = (jnp.max(most) > ROOM).astype(jnp.int32)
+
+
+def fast_kernel(level_no, picked_ref, slot_ref, *refs):
+    answer_refs, row_refs, out_ref = refs[:level_no], refs[level_no:-1], refs[-1]
+    tiles, room, count = row_refs[0].shape
+    total = jnp.zeros((answer_refs[0].shape[0], tiles * room), F32)
+    for answer_ref, row_ref in zip(answer_refs, row_refs):
+        total = total + dot_nt(answer_ref[...], row_ref[...].reshape(tiles * room, count))
+    high = total.astype(BF16)
+    low = (total - high.astype(F32)).astype(BF16)
+    chosen = equal_rows(tiles * room, slot_ref[level_no - 1], BF16)
+    change = dot_nn(high, chosen) + dot_nn(low, chosen)
+    store_copies((picked_ref[...].astype(F32) - change).astype(BF16), out_ref)
+
+
+def copy_kernel(*refs):
+    share = refs[0].shape[0]
+    for spot, value_ref in enumerate(refs[:-1]):
+        for copy in range(refs[-1].shape[0]):
+            refs[-1][copy, spot * share : (spot + 1) * share, :] = value_ref[...]
+
+
+def tile_kernel(lift_ref, answer_ref, out_ref):
+    blocks, rows, count = answer_ref.shape
+    share = out_ref.shape[1]
+    total = jnp.zeros((lift_ref.shape[1], blocks * share), F32)
+    for earlier in range(rows // share):
+        answer = answer_ref[:, earlier * share : (earlier + 1) * share, :]
+        total = total + dot_nt(lift_ref[earlier], answer.reshape(blocks * share, count))
+    send_field(total, out_ref)
+
+
+def less_kernel(level_no, picked_ref, recv_ref, skeleton_ref, out_ref):
+    change = pick_rows(recv_ref[...], skeleton_ref[level_no])
+    store_copies((picked_ref[...].astype(F32) - change).astype(BF16), out_ref)
 
 
 def solve_kernel(level_no, leaf_ref, nodes_ref, coupling_ref, inverse_ref, *refs):
@@ -217,7 +271,20 @@
     first = (lax.axis_index("blk") // CELL * CELL).astype(jnp.int32).reshape(1)
     cells = [list(range(c, c + CELL)) for c in range(0, blk_count, CELL)]
 
-    lifts = [lax.all_gather(lift[level_no], "blk", axis=0) for level_no in range(LEVELS - 1)]
+    tile_no = lax.axis_index("blk").astype(jnp.int32).reshape(1)
+    pairs = LEVELS * (LEVELS - 1) // 2
+    rows, slot_of, over = pl.pallas_call(
+        lambda *refs: plan_kernel(blk_count, *refs),
+        out_shape=(
+            jax.ShapeDtypeStruct((pairs * ROOM, slots), BF16),
+            jax.ShapeDtypeStruct((LEVELS - 1, 1, slots), jnp.int32),
+            jax.ShapeDtypeStruct((1,), jnp.int32),
+        ),
+        in_specs=[SMEM, VMEM, VMEM],
+        out_specs=(VMEM, VMEM, SMEM),
+        name="plan",
+    )(tile_no, skeleton, lift)
+    rows = lax.all_gather(rows, "blk", axis=0)
     packed = pl.pallas_call(
         pack_kernel,
         out_shape=jax.ShapeDtypeStruct((blk_count, block + EXTRA, pts), BF16),
@@ -247,6 +314,56 @@
     )(near, right_side, iterate, leaf_inverse)
 
     sent = lax.all_to_all(sent, "blk", 0, 0)
+    small_shape = jax.ShapeDtypeStruct((share, slots), BF16)
+    picked = pl.pallas_call(
+        pick_kernel,
+        out_shape=(small_shape,) * LEVELS,
+        in_specs=[VMEM] * 2,
+        out_specs=(VMEM,) * LEVELS,
+        name="pick",
+    )(sent, skeleton)
+
+    def fast(level_no, shape, answers):
+        offset = level_no * (level_no - 1) // 2
+        return pl.pallas_call(
+            lambda *refs: fast_kernel(level_no, *refs),
+            out_shape=shape,
+            grid=(1,),
+            in_specs=[whole_spec((share, slots)), whole_spec(slot_of.shape)]
+            + [whole_spec((share, slots))] * level_no
+            + [
+                pl.BlockSpec((blk_count, ROOM, slots), lambda step, spot=offset + k: (0, spot, 0))
+                for k in range(level_no)
+            ],
+            out_specs=whole_spec(shape.shape),
+            name="fast",
+        )(picked[level_no], slot_of, *answers, *[rows] * level_no)
+
+    def slow(level_no, shape, answers):
+        copies = pl.pallas_call(
+            copy_kernel,
+            out_shape=jax.ShapeDtypeStruct((blk_count, level_no * share, slots), BF16),
+            in_specs=[VMEM] * level_no,
+            out_specs=VMEM,
+            name="copies",
+        )(*answers)
+        copies = lax.all_to_all(copies, "blk", 0, 0)
+        change = pl.pallas_call(
+            tile_kernel,
+            out_shape=send_shape,
+            in_specs=[VMEM] * 2,
+            out_specs=VMEM,
+            name="tile",
+        )(lift, copies)
+        change = lax.all_to_all(change, "blk", 0, 0)
+        return pl.pallas_call(
+            lambda *refs: less_kernel(level_no, *refs),
+            out_shape=shape,
+            in_specs=[VMEM] * 3,
+            out_specs=VMEM,
+            name="less",
+        )(picked[level_no], change, skeleton)
+
     answers = []
     for level_no in range(LEVELS):
         last = level_no == LEVELS - 1
@@ -254,30 +371,16 @@
         groups = [list(range(c, c + width)) for c in range(0, leaf_count, width)]
         spread = level_no == 2
         node_shape = (width, share, slots)
-        pick_shape = jax.ShapeDtypeStruct(node_shape if spread else node_shape[1:], BF16)
         if level_no == 0:
-            nodes = pl.pallas_call(
-                pick_kernel,
-                out_shape=pick_shape,
-                in_specs=[VMEM] * 2,
-                out_specs=VMEM,
-                name="pick",
-            )(sent, skeleton)
+            nodes = picked[0]
         else:
-            kept_shape = jax.ShapeDtypeStruct(sent.shape, F32)
-            sent, nodes = pl.pallas_call(
-                lambda *refs, level_no=level_no - 1: update_kernel(level_no, *refs),
-                out_shape=(kept_shape, pick_shape),
-                grid=(blk_count // CELL,),
-                in_specs=[
-                    whole_spec(sent.shape),
-                    whole_spec((share, slots)),
-                    pl.BlockSpec((CELL, pts, slots), lambda step: (step, 0, 0)),
-                    whole_spec(skeleton.shape),
-                ],
-                out_specs=(whole_spec(kept_shape.shape), whole_spec(pick_shape.shape)),
-                name="update",
-            )(sent, answers[-1], lifts[level_no - 1], skeleton)
+            pick_shape = jax.ShapeDtypeStruct(node_shape if spread else node_shape[1:], BF16)
+            nodes = lax.cond(
+                over[0] > 0,
+                lambda *given, level_no=level_no: slow(level_no, pick_shape, given),
+                lambda *given, level_no=level_no: fast(level_no, pick_shape, given),
+                *answers,
+            )
         if spread:
             nodes = lax.all_to_all(nodes, "leaf", 0, 0, axis_index_groups=groups)
         else:

time: 258 us -> 187 us (0.72)
  waiting for transfers between devices: 114 us -> 50.4 us
  Pallas kernels: 35.3 us -> 30.5 us
    all_gather x2 -> x1, waiting for transfers between devices: 61 us -> 0.01 us  [on_device(): rows = lax.all_gather(rows, 'blk', axis=0)]
    pallas_call x3 -> x4, Pallas kernels: 11.2 us -> 7.67 us  [the longest x2 3.01 us: fast(): pl.pallas_call(lambda *refs: fast_kernel(level_no, *refs), out_shape=shap...]
  transfers between devices with their start and end apart: 4 -> 3, of which waited for: 3 -> 2; matrix products, arithmetic and copies ran while one was open for 0% -> 0% of each run, Pallas kernels for 10% -> 10%
where the time goes in v3:
time: 187 us; the launch traced here: 186 us
  blocking collectives  64.2 us (34%)
  waiting for transfers between devices  50.4 us (27%)
  Pallas kernels  30.5 us (16%)
  starting transfers between devices  24.8 us (13%)
  between operations  14 us (7%)
  local copies, waits for them, and re-layouts  1.93 us (1%)
    all_to_all x1, waiting for transfers between devices, on_device(): packed = lax.all_to_all(packed, 'blk', 0, 0)  36.7 us
    all_gather x1, blocking collectives, on_device(): answer = lax.all_gather(answers[-1], 'blk', axis=0)  34.9 us
    all_to_all x1, starting transfers between devices, on_device(): packed = lax.all_to_all(packed, 'blk', 0, 0)  15.3 us
    all_to_all x1, waiting for transfers between devices, on_device(): sent = lax.all_to_all(sent, 'blk', 0, 0)  13.7 us
    pallas_call x1, Pallas kernels, on_device(): pl.pallas_call(near_kernel, out_shape=jax.ShapeDtypeStruct((CELL, block,...  10.7 us
    all_to_all x1, blocking collectives, on_device(): nodes = lax.all_to_all(nodes, 'leaf', 0, 0, axis_index_groups=groups)  10.5 us
    all_to_all x1, blocking collectives, on_device(): near = lax.all_to_all(near, 'blk', 0, 0, axis_index_groups=cells)  10 us
    all_to_all x1, starting transfers between devices, on_device(): sent = lax.all_to_all(sent, 'blk', 0, 0)  9.45 us
  transfers between devices with their start and end apart: 3, of which 2 were waited for; matrix products, arithmetic and copies ran while one was open for 0% of the time, Pallas kernels for 10%

profile of v3, /device:TPU:6, one launch (start us, length us, event | category | flops | bytes accessed | tf_op | source)
XLA Modules:
  0.0 185.9 jit_solution(15383293265075036786)
XLA Ops:
  6.5 2.9 %plan.1 = (bf16[192,512]{1,0:T(8,128)(2,1)}, s32[2,1,512]{2,1,0:T(1,128)S(1)}, s32[1]{0:T(128)}) custom-call(s32[1]{0:T(128)} %bitcast.2.refs_0_, s32[3,1,512]{2,1,0:T(1,128)} %skeleton_ref.1, bf16[3,256,512]{2,1,0:T(8,128)(2,1)} %lift_ref.1), custom_call_target="tpu_custom_call" | custom-call | tf_op jit(solution)/shard_map/plan/pallas_call | solution.py:276
  9.5 1.8 pack.1
  11.3 15.3 %all-to-all-start.4 = ((bf16[16,72,256]{2,1,0:T(8,128)(2,1)}), bf16[16,72,256]{2,1,0:T(8,128)(2,1)S(1)}, u32[]{:S(2)}, u32[]{:S(2)}) async-start(bf16[16,72,256]{2,1,0:T(8,128)(2,1)} %pack.1), calls=%async_computation.4 | async-start | bytes 1179648 | tf_op jit(solution)/shard_map/all_to_all | solution.py:296
  26.7 36.7 %all-to-all-done.4.recv_ref = bf16[16,72,256]{2,1,0:T(8,128)(2,1)S(1)} async-done(((bf16[16,72,256]{2,1,0:T(8,128)(2,1)}), bf16[16,72,256]{2,1,0:T(8,128)(2,1)S(1)}, u32[]{:S(2)}, u32[]{:S(2)}) %all-to-all-start.4) | async-done | bytes 589856 | tf_op jit(solution)/shard_map/all_to_all | solution.py:296
  63.3 0.8 copy-done.4
  64.1 10.7 %near.1 = bf16[4,64,256]{2,1,0:T(8,128)(2,1)} custom-call(s32[1]{0:T(128)} %bitcast.cell_ref, bf16[16,72,256]{2,1,0:T(8,128)(2,1)} %copy-done.4), custom_call_target="tpu_custom_call" | custom-call | tf_op jit(solution)/shard_map/near/pallas_call | solution.py:297
  74.9 10.0 %all_to_all.40.near_ref = bf16[4,64,256]{2,1,0:T(8,128)(2,1)} all-to-all(bf16[4,64,256]{2,1,0:T(8,128)(2,1)} %near.1), channel_id=1, replica_groups={{0,1,2,3},{4,5,6,7},{8,9,10,11},{12,13,14,15},{16,17,18,19},{20,21,22,2..., dimensions={0} | all-to-all | bytes 262144 | tf_op jit(solution)/shard_map/all_to_all | solution.py:305
  84.9 2.1 %leaf.1 = (f32[256,256]{1,0:T(8,128)}, bf16[16,16,256]{2,1,0:T(8,128)(2,1)}) custom-call(bf16[4,64,256]{2,1,0:T(8,128)(2,1)} %all_to_all.40.near_ref, f32[256,256]{1,0:T(8,128)} %right_ref.1, bf16[256,256]{1,0:T(8,128)(2,1)} %iterate_ref.3, bf16[1,256,256]{2,1,0:T(8,128)(2,1)} %inverse_ref.1), custom_call_target="tpu_custom_call" | custom-call | tf_op jit(solution)/shard_map/leaf/pallas_call | solution.py:308
  87.1 9.5 %all-to-all-start.6 = ((bf16[16,16,256]{2,1,0:T(8,128)(2,1)}), bf16[16,16,256]{2,1,0:T(8,128)(2,1)S(1)}, u32[]{:S(2)}, u32[]{:S(2)}) async-start(bf16[16,16,256]{2,1,0:T(8,128)(2,1)} %get-tuple-element.75), calls=%async_computation.6 | async-start | bytes 262144 | tf_op jit(solution)/shard_map/all_to_all | solution.py:316
  97.1 13.7 %all-to-all-done.6.recv_ref = bf16[16,16,256]{2,1,0:T(8,128)(2,1)S(1)} async-done(((bf16[16,16,256]{2,1,0:T(8,128)(2,1)}), bf16[16,16,256]{2,1,0:T(8,128)(2,1)S(1)}, u32[]{:S(2)}, u32[]{:S(2)}) %all-to-all-start.6) | async-done | bytes 131104 | tf_op jit(solution)/shard_map/all_to_all | solution.py:316
  110.8 0.6 copy-done.5
  111.4 1.8 pick.1
  113.2 3.1 %all-gather = bf16[32,512]{1,0:T(8,128)(2,1)} all-gather(bf16[16,512]{1,0:T(8,128)(2,1)} %get-tuple-element.78), channel_id=2, replica_groups={{0,16},{32,48},{64,80},{96,112},{128,144},{160,176},{192,208},{224,240}..., dimensions={0}, use_global_device_ids=true | all-gather | bytes 49152 | tf_op jit(solution)/shard_map/all_gather | solution.py:387
  116.3 1.7 solve.3.refs_4_
  118.0 2.0 %conditional.2 = (bf16[16,512]{1,0:T(8,128)(2,1)S(1)}) conditional(s32[]{:T(128)} %bitcast.3, (bf16[16,512]{1,0:T(8,128)(2,1)S(1)}, s32[2,1,512]{2,1,0:T(1,128)S(1)}, bf16[16,512]{1,0:T(8,128)(2,1)S(1)}, bf16[16,192,512]{2,1,0:T(8,128)(2,1)}) %tuple.27, (bf16[16,512]{1,0:T(8,128)(2,1)S(1)}, bf16[3,256,512]{2,1,0:T(8,128)(2,1)S(1)}, ...), branch_computations={%region_0.1_spmd, %region_1.2_spmd} | conditional | bytes 786440 | solution.py:378
  118.0 2.0 %fast.2 = bf16[16,512]{1,0:T(8,128)(2,1)S(1)} custom-call(bf16[16,512]{1,0:T(8,128)(2,1)S(1)} %get-tuple-element.46.refs_0_, s32[2,1,512]{2,1,0:T(1,128)S(1)} %get-tuple-element.48.refs_1_, bf16[16,512]{1,0:T(8,128)(2,1)S(1)} %get-tuple-element.49.refs_2_, bf16[16,192,512]{2,1,0:T(8,128)(2,1)} %get-tuple-element.50.refs_3_), custom_call_target="tpu_custom_call" | custom-call | tf_op jit(solution)/shard_map/cond/branch_0_fun/fast/pallas_call | solution.py:328
  120.0 5.7 %all-gather.2 = bf16[64,512]{1,0:T(8,128)(2,1)} all-gather(bf16[16,512]{1,0:T(8,128)(2,1)S(1)} %get-tuple-element.81), channel_id=4, replica_groups={{0,16,32,48},{64,80,96,112},{128,144,160,176},{192,208,224,240},{256,27..., dimensions={0}, use_global_device_ids=true | all-gather | bytes 81920 | tf_op jit(solution)/shard_map/all_gather | solution.py:387
  125.7 1.8 solve.4.refs_5_
  127.9 1.0 conditional.3
  127.9 1.0 fast.3
  129.0 10.5 %all_to_all.41.refs_1_ = bf16[8,16,512]{2,1,0:T(8,128)(2,1)} all-to-all(bf16[8,16,512]{2,1,0:T(8,128)(2,1)S(1)} %get-tuple-element.82), channel_id=1, replica_groups={{0,16,32,48,64,80,96,112},{128,144,160,176,192,208,224,240},{256,272,28..., dimensions={0} | all-to-all | bytes 262144 | tf_op jit(solution)/shard_map/all_to_all | solution.py:385
  139.5 2.4 %solve.5 = bf16[48,512]{1,0:T(8,128)(2,1)} custom-call(s32[1]{0:T(128)} %bitcast.1.refs_0_, bf16[8,16,512]{2,1,0:T(8,128)(2,1)} %all_to_all.41.refs_1_, bf16[3,1,512,512]{3,2,1,0:T(8,128)(2,1)} %refs_2_.7, bf16[3,1,512,512]{3,2,1,0:T(8,128)(2,1)} %refs_3_.5, bf16[16,512]{1,0:T(8,128)(2,1)S(1)} %solve.3.refs_4_, bf16[16,512]{1,0:T(8,128)(2,1)S(1)} %solve.4.refs_5_), custom_call_target="tpu_custom_call" | custom-call | tf_op jit(solution)/shard_map/solve/pallas_call | solution.py:390
  141.8 34.9 %all-gather.3 = bf16[768,512]{1,0:T(8,128)(2,1)} all-gather(bf16[48,512]{1,0:T(8,128)(2,1)} %solve.5), channel_id=5, replica_groups=mesh['leaf'=32,'blk'=16] {'blk'}, dimensions={0}, use_global_device_ids=true | all-gather | bytes 835584 | tf_op jit(solution)/shard_map/all_gather | solution.py:405
  176.7 2.3 %lift.1 = f32[256,256]{1,0:T(8,128)} custom-call(f32[256,256]{1,0:T(8,128)} %get-tuple-element.73.field_ref, bf16[3,256,512]{2,1,0:T(8,128)(2,1)S(1)} %copy-done.2, bf16[16,48,512]{2,1,0:T(8,128)(2,1)} %bitcast.10), custom_call_target="tpu_custom_call" | custom-call | tf_op jit(solution)/shard_map/lift/pallas_call | solution.py:406
  (13 shorter events, 0.5 us)
Async XLA Ops:
  6.5 111.5 %all-gather.6.cloned.1.call-start = ((), (), s32[]{:S(2)}) async-start(), calls=%async_computation.8 | async-start | bytes 3342336 | tf_op jit(solution)/shard_map/all_gather | solution.py:287
  11.3 100.1 %copy-start.6 = (s32[3,1,512]{2,1,0:T(1,128)S(1)}, s32[3,1,512]{2,1,0:T(1,128)}, u32[]{:S(2)}) copy-start(s32[3,1,512]{2,1,0:T(1,128)} %skeleton_ref.1) | copy-start | bytes 18436
  11.3 52.0 %all-to-all-start.4 = ((bf16[16,72,256]{2,1,0:T(8,128)(2,1)}), bf16[16,72,256]{2,1,0:T(8,128)(2,1)S(1)}, u32[]{:S(2)}, u32[]{:S(2)}) async-start(bf16[16,72,256]{2,1,0:T(8,128)(2,1)} %pack.1), calls=%async_computation.4 | async-start | bytes 1179648 | tf_op jit(solution)/shard_map/all_to_all | solution.py:296
  63.3 0.8 copy-start.4
  87.1 23.7 %all-to-all-start.6 = ((bf16[16,16,256]{2,1,0:T(8,128)(2,1)}), bf16[16,16,256]{2,1,0:T(8,128)(2,1)S(1)}, u32[]{:S(2)}, u32[]{:S(2)}) async-start(bf16[16,16,256]{2,1,0:T(8,128)(2,1)} %get-tuple-element.75), calls=%async_computation.6 | async-start | bytes 262144 | tf_op jit(solution)/shard_map/all_to_all | solution.py:316
  110.8 0.6 copy-start.5
  116.3 1.7 copy-start.1
  125.7 2.2 %copy-start = (bf16[3072,512]{1,0:T(8,128)(2,1)S(1)}, bf16[3072,512]{1,0:T(8,128)(2,1)}, u32[]{:S(2)}) copy-start(bf16[3072,512]{1,0:T(8,128)(2,1)} %all-gather.6.cloned.1.call-done) | copy-start | bytes 9437188
  139.5 37.2 %copy-start.2 = (bf16[3,256,512]{2,1,0:T(8,128)(2,1)S(1)}, bf16[3,256,512]{2,1,0:T(8,128)(2,1)}, u32[]{:S(2)}) copy-start(bf16[3,256,512]{2,1,0:T(8,128)(2,1)} %lift_ref.1) | copy-start | bytes 2359300
Sparse Core Ops, SparseCore 0:
  9.6 101.2 all-gather.5

commit v4 on v3

--- a/solution.py
+++ b/solution.py
@@ -8,8 +8,10 @@
 from jax.sharding import PartitionSpec as P
 
 LEVELS = 3
-CELL = 4
+CELL = 8
+CHUNK = 1024
 ROOM = 64
+KERNEL_BYTES = 16 << 20
 
 kernel_scale = 0.125
 spread_coef = 4.0
@@ -22,6 +24,7 @@
 
 F32 = jnp.float32
 BF16 = jnp.bfloat16
+PARAMS = pltpu.CompilerParams(vmem_limit_bytes=KERNEL_BYTES)
 VMEM = pl.BlockSpec(memory_space=pltpu.VMEM)
 SMEM = pl.BlockSpec(memory_space=pltpu.SMEM)
 
@@ -62,14 +65,14 @@
         out_ref[dest, block:rows, :] = extra
 
 
-def near_kernel(cell_ref, recv_ref, out_ref, acc_ref):
+def near_kernel(cell_ref, recv_ref, out_ref, acc_ref, left_ref):
     count, rows, pts = recv_ref.shape
     block = rows - EXTRA
     first = cell_ref[0]
     row_no = lax.broadcasted_iota(jnp.int32, (EXTRA, pts), 0)
-    lane_no = lax.broadcasted_iota(jnp.int32, (EXTRA, pts), 1)
     coord_rows = (row_no % 4) != 3
     three_rows = row_no < 3
+    ones = jnp.where(three_rows, 1.0, 0.0)
 
     def coords(extra):
         whole = jnp.where(coord_rows, extra + pltpu.roll(extra, 4, 0), 0.0)
@@ -82,33 +85,35 @@
         return jnp.where(three_rows, jnp.where(row_no == 0, high, picked), 0.0)
 
     left = []
-    masks = []
+    cell_rows = lax.broadcasted_iota(jnp.int32, (CELL, pts), 0)
+    tile_no = lax.broadcasted_iota(jnp.int32, (CELL, pts), 1)
+    masks = jnp.zeros((CELL, pts), F32)
     for member in range(CELL):
         extra = recv_ref[first + member, block:rows, :].astype(F32)
-        masks.append(extra[3:4, :])
+        masks = jnp.where(cell_rows == member, extra[3:4, :], masks)
         whole, square = coords(extra)
         parts = split_parts(2.0 * EXP2_COEF * whole)
         own = split_parts(EXP2_BASE - EXP2_COEF * square)
-        unit = jnp.where(three_rows | (row_no == 3 + member), 1.0, 0.0)
-        left.append(jnp.concatenate([*parts, rows_of(own), unit], axis=0))
-    left = jnp.concatenate(left, axis=1).astype(BF16)
-    ones = jnp.where(three_rows, 1.0, 0.0)
+        unit = jnp.where(cell_rows == member, 1.0, 0.0)
+        value = jnp.concatenate([*parts, rows_of(own), ones, unit], axis=0).astype(BF16)
+        left_ref[:, member * pts : (member + 1) * pts] = value
     acc_ref[...] = jnp.zeros_like(acc_ref)
 
     def step(tile, carry):
         extra = recv_ref[tile, block:rows, :].astype(F32)
         whole, square = coords(extra)
         tail = rows_of(split_parts(-EXP2_COEF * square))
-        for member in range(CELL):
-            chosen = jnp.where(lane_no[0:1] == tile, masks[member], 0.0)
-            flag = jnp.sum(chosen, axis=1, keepdims=True)
-            tail = jnp.where(row_no == 3 + member, (flag - 1.0) * OFF_BIAS, tail)
-        right = jnp.concatenate([extra, extra, extra, ones, tail], axis=0).astype(BF16)
-        value = jnp.exp2(dot_tn(right, left)).astype(BF16)
-        acc_ref[...] += dot_nn(recv_ref[tile, 0:block, :], value)
+        flag = jnp.sum(jnp.where(tile_no == tile, masks, 0.0), axis=1, keepdims=True)
+        bias = jnp.broadcast_to((flag - 1.0) * OFF_BIAS, masks.shape)
+        right = jnp.concatenate([extra, extra, extra, ones, tail, bias], axis=0).astype(BF16)
+        iterate = recv_ref[tile, 0:block, :]
+        for low in range(0, CELL * pts, CHUNK):
+            span = slice(low, low + CHUNK)
+            value = jnp.exp2(dot_tn(right, left_ref[:, span])).astype(BF16)
+            acc_ref[:, span] += dot_nn(iterate, value)
         return carry
 
-    lax.fori_loop(0, count, step, 0)
+    lax.fori_loop(0, count, step, 0, unroll=2)
     for member in range(CELL):
         out_ref[member] = acc_ref[:, member * pts : (member + 1) * pts].astype(BF16)
 
@@ -269,9 +274,12 @@
     block = cols // CELL
     leaf_no = lax.axis_index("leaf").astype(jnp.int32).reshape(1)
     first = (lax.axis_index("blk") // CELL * CELL).astype(jnp.int32).reshape(1)
+    tile_no = lax.axis_index("blk").astype(jnp.int32).reshape(1)
     cells = [list(range(c, c + CELL)) for c in range(0, blk_count, CELL)]
-
-    tile_no = lax.axis_index("blk").astype(jnp.int32).reshape(1)
+    leaf_no, first, tile_no, points, skeleton = lax.optimization_barrier(
+        (leaf_no, first, tile_no, points, skeleton)
+    )
+
     pairs = LEVELS * (LEVELS - 1) // 2
     rows, slot_of, over = pl.pallas_call(
         lambda *refs: plan_kernel(blk_count, *refs),
@@ -282,6 +290,7 @@
         ),
         in_specs=[SMEM, VMEM, VMEM],
         out_specs=(VMEM, VMEM, SMEM),
+        compiler_params=PARAMS,
         name="plan",
     )(tile_no, skeleton, lift)
     rows = lax.all_gather(rows, "blk", axis=0)
@@ -291,6 +300,7 @@
         in_specs=[VMEM] * 3,
         out_specs=VMEM,
         scratch_shapes=[pltpu.VMEM((EXTRA, pts), F32)],
+        compiler_params=PARAMS,
         name="pack",
     )(points, iterate, near_mask)
     packed = lax.all_to_all(packed, "blk", 0, 0)
@@ -299,7 +309,11 @@
         out_shape=jax.ShapeDtypeStruct((CELL, block, pts), BF16),
         in_specs=[SMEM, VMEM],
         out_specs=VMEM,
-        scratch_shapes=[pltpu.VMEM((block, CELL * pts), F32)],
+        scratch_shapes=[
+            pltpu.VMEM((block, CELL * pts), F32),
+            pltpu.VMEM((5 * EXTRA + CELL, CELL * pts), BF16),
+        ],
+        compiler_params=PARAMS,
         name="near",
     )(first, packed)
     near = lax.all_to_all(near, "blk", 0, 0, axis_index_groups=cells)
@@ -310,16 +324,19 @@
         out_shape=(field_shape, send_shape),
         in_specs=[VMEM] * 4,
         out_specs=(VMEM, VMEM),
+        compiler_params=PARAMS,
         name="leaf",
     )(near, right_side, iterate, leaf_inverse)
 
     sent = lax.all_to_all(sent, "blk", 0, 0)
+    sent, over = lax.optimization_barrier((sent, over))
     small_shape = jax.ShapeDtypeStruct((share, slots), BF16)
     picked = pl.pallas_call(
         pick_kernel,
         out_shape=(small_shape,) * LEVELS,
         in_specs=[VMEM] * 2,
         out_specs=(VMEM,) * LEVELS,
+        compiler_params=PARAMS,
         name="pick",
     )(sent, skeleton)
 
@@ -336,6 +353,7 @@
                 for k in range(level_no)
             ],
             out_specs=whole_spec(shape.shape),
+            compiler_params=PARAMS,
             name="fast",
         )(picked[level_no], slot_of, *answers, *[rows] * level_no)
 
@@ -345,6 +363,7 @@
             out_shape=jax.ShapeDtypeStruct((blk_count, level_no * share, slots), BF16),
             in_specs=[VMEM] * level_no,
             out_specs=VMEM,
+            compiler_params=PARAMS,
             name="copies",
         )(*answers)
         copies = lax.all_to_all(copies, "blk", 0, 0)
@@ -353,6 +372,7 @@
             out_shape=send_shape,
             in_specs=[VMEM] * 2,
             out_specs=VMEM,
+            compiler_params=PARAMS,
             name="tile",
         )(lift, copies)
         change = lax.all_to_all(change, "blk", 0, 0)
@@ -361,6 +381,7 @@
             out_shape=shape,
             in_specs=[VMEM] * 3,
             out_specs=VMEM,
+            compiler_params=PARAMS,
             name="less",
         )(picked[level_no], change, skeleton)
 
@@ -399,6 +420,7 @@
             ]
             + [whole_spec((share, slots))] * len(earlier),
             out_specs=whole_spec(answer_shape),
+            compiler_params=PARAMS,
             name="solve",
         )(leaf_no, nodes, coupling, reduced_inverse, *earlier)
         answers.append(answer)
@@ -408,6 +430,7 @@
         out_shape=field_shape,
         in_specs=[VMEM] * 3,
         out_specs=VMEM,
+        compiler_params=PARAMS,
         name="lift",
     )(field, lift, answer)
 

time: 187 us -> 170 us (0.909)
  blocking collectives: 64.2 us -> 130 us
  waiting for transfers between devices: 50.4 us -> 0.02 us
  starting transfers between devices: 24.8 us -> 0.01 us
  Pallas kernels: 30.5 us -> 20.4 us
  local copies, waits for them, and re-layouts: 1.93 us -> 5.47 us
    all_to_all x0 -> x2, blocking collectives: none -> 60.3 us  [the longest x1 39.4 us: on_device(): packed = lax.all_to_all(packed, 'blk', 0, 0)]
    all_to_all x2 -> x0, waiting for transfers between devices: 50.3 us -> none  [the longest x1 36.7 us: on_device(): packed = lax.all_to_all(packed, 'blk', 0, 0)]
    all_to_all x2 -> x0, starting transfers between devices: 24.8 us -> none  [the longest x1 15.3 us: on_device(): packed = lax.all_to_all(packed, 'blk', 0, 0)]
    all_to_all x1, blocking collectives: 10 us -> 18.7 us  [on_device(): near = lax.all_to_all(near, 'blk', 0, 0, axis_index_groups=cells)]
    pallas_call x3, Pallas kernels: 5.82 us -> 1.21 us  [on_device(): pl.pallas_call(lambda *refs, level_no=level_no: solve_kernel(level_no, *r...]
    unnamed x12 -> x28, local copies, waits for them, and re-layouts: 1.93 us -> 5.47 us
  transfers between devices with their start and end apart: 3 -> 1, of which waited for: 2 -> 0; matrix products, arithmetic and copies ran while one was open for 0% -> 0% of each run, Pallas kernels for 10% -> 7%
where the time goes in v4:
time: 170 us
  blocking collectives  130 us (76%)
  Pallas kernels  20.4 us (12%)
  between operations  14.1 us (8%)
  local copies, waits for them, and re-layouts  5.47 us (3%)
    all_to_all x1, blocking collectives, on_device(): packed = lax.all_to_all(packed, 'blk', 0, 0)  39.4 us
    all_gather x1, blocking collectives, on_device(): answer = lax.all_gather(answers[-1], 'blk', axis=0)  33.1 us
    all_to_all x1, blocking collectives, on_device(): sent = lax.all_to_all(sent, 'blk', 0, 0)  20.8 us
    all_to_all x1, blocking collectives, on_device(): near = lax.all_to_all(near, 'blk', 0, 0, axis_index_groups=cells)  18.7 us
    pallas_call x1, Pallas kernels, on_device(): pl.pallas_call(near_kernel, out_shape=jax.ShapeDtypeStruct((CELL, block,...  11.5 us
    all_to_all x1, blocking collectives, on_device(): nodes = lax.all_to_all(nodes, 'leaf', 0, 0, axis_index_groups=groups)  10.8 us
    all_gather x2, blocking collectives, on_device(): nodes = lax.all_gather(nodes, 'leaf', axis=0, axis_index_groups=groups)  7.06 us
    unnamed x28, local copies, waits for them, and re-layouts  5.47 us
  transfers between devices with their start and end apart: 1, of which 0 were waited for; matrix products, arithmetic and copies ran while one was open for 0% of the time, Pallas kernels for 7%

profile of v4, /device:TPU:6, one launch (start us, length us, event | category | flops | bytes accessed | tf_op | source)
XLA Modules:
  0.0 169.9 jit_solution(6046861459945336437)
XLA Ops:
  6.5 2.7 %plan.1 = (bf16[192,512]{1,0:T(8,128)(2,1)S(1)}, s32[2,1,512]{2,1,0:T(1,128)S(1)}, s32[1]{0:T(128)}) custom-call(s32[1]{0:T(128)} %bitcast.2.refs_0_, s32[3,1,512]{2,1,0:T(1,128)} %skeleton_ref, bf16[3,256,512]{2,1,0:T(8,128)(2,1)} %lift_ref.1), custom_call_target="tpu_custom_call" | custom-call | tf_op jit(solution)/shard_map/plan/pallas_call | solution.py:284
  9.2 0.7 copy-done.7
  9.9 1.0 copy-done.2
  11.0 0.7 copy-done.9
  11.7 0.7 copy-done.10
  12.4 39.4 %all_to_all.40.recv_ref = bf16[16,40,256]{2,1,0:T(8,128)(2,1)S(1)} all-to-all(bf16[16,40,256]{2,1,0:T(8,128)(2,1)S(1)} %pack.1), channel_id=1, replica_groups=mesh['leaf'=32,'blk'=16] {'blk'}, dimensions={0} | all-to-all | bytes 655360 | tf_op jit(solution)/shard_map/all_to_all | solution.py:306
  51.8 11.5 %near.1 = bf16[8,32,256]{2,1,0:T(8,128)(2,1)S(1)} custom-call(s32[1]{0:T(128)} %bitcast.1.cell_ref, bf16[16,40,256]{2,1,0:T(8,128)(2,1)S(1)} %all_to_all.40.recv_ref), custom_call_target="tpu_custom_call" | custom-call | tf_op jit(solution)/shard_map/near/pallas_call | solution.py:307
  63.3 18.7 %all_to_all.41.near_ref = bf16[8,32,256]{2,1,0:T(8,128)(2,1)S(1)} all-to-all(bf16[8,32,256]{2,1,0:T(8,128)(2,1)S(1)} %near.1), channel_id=1, replica_groups={{0,1,2,3,4,5,6,7},{8,9,10,11,12,13,14,15},{16,17,18,19,20,21,22,23},{24..., dimensions={0} | all-to-all | bytes 262144 | tf_op jit(solution)/shard_map/all_to_all | solution.py:319
  82.1 0.9 copy-done.8
  83.3 20.8 %all_to_all.42.recv_ref = bf16[16,16,256]{2,1,0:T(8,128)(2,1)S(1)} all-to-all(bf16[16,16,256]{2,1,0:T(8,128)(2,1)S(1)} %get-tuple-element.84), channel_id=1, replica_groups=mesh['leaf'=32,'blk'=16] {'blk'}, dimensions={0} | all-to-all | bytes 262144 | tf_op jit(solution)/shard_map/all_to_all | solution.py:331
  104.8 0.4 pick.1
  105.2 1.8 %all-gather = bf16[32,512]{1,0:T(8,128)(2,1)S(1)} all-gather(bf16[16,512]{1,0:T(8,128)(2,1)S(1)} %get-tuple-element.92), channel_id=2, replica_groups={{0,16},{32,48},{64,80},{96,112},{128,144},{160,176},{192,208},{224,240}..., dimensions={0}, use_global_device_ids=true | all-gather | bytes 49152 | tf_op jit(solution)/shard_map/all_gather | solution.py:408
  107.0 0.4 solve.3.refs_4_
  107.4 2.0 %conditional.2 = (bf16[16,512]{1,0:T(8,128)(2,1)S(1)}) conditional(s32[]{:T(128)} %bitcast.3, (bf16[16,512]{1,0:T(8,128)(2,1)S(1)}, s32[2,1,512]{2,1,0:T(1,128)S(1)}, bf16[16,512]{1,0:T(8,128)(2,1)S(1)}, bf16[16,192,512]{2,1,0:T(8,128)(2,1)}) %tuple.31, (bf16[16,512]{1,0:T(8,128)(2,1)S(1)}, bf16[3,256,512]{2,1,0:T(8,128)(2,1)}, ...), branch_computations={%region_0.1_spmd, %region_1.2_spmd} | conditional | bytes 786440 | solution.py:399
  107.4 2.0 %fast.2 = bf16[16,512]{1,0:T(8,128)(2,1)S(1)} custom-call(bf16[16,512]{1,0:T(8,128)(2,1)S(1)} %get-tuple-element.46.refs_0_, s32[2,1,512]{2,1,0:T(1,128)S(1)} %get-tuple-element.48.refs_1_, bf16[16,512]{1,0:T(8,128)(2,1)S(1)} %get-tuple-element.49.refs_2_, bf16[16,192,512]{2,1,0:T(8,128)(2,1)} %get-tuple-element.50.refs_3_), custom_call_target="tpu_custom_call" | custom-call | tf_op jit(solution)/shard_map/cond/branch_0_fun/fast/pallas_call | solution.py:345
  109.5 5.2 %all-gather.2 = bf16[64,512]{1,0:T(8,128)(2,1)S(1)} all-gather(bf16[16,512]{1,0:T(8,128)(2,1)S(1)} %get-tuple-element.95), channel_id=4, replica_groups={{0,16,32,48},{64,80,96,112},{128,144,160,176},{192,208,224,240},{256,27..., dimensions={0}, use_global_device_ids=true | all-gather | bytes 81920 | tf_op jit(solution)/shard_map/all_gather | solution.py:408
  114.7 0.4 solve.4.refs_5_
  115.1 1.5 copy-done.11
  116.6 1.0 conditional.3
  116.6 1.0 fast.3
  117.6 10.8 %all_to_all.43.refs_1_ = bf16[8,16,512]{2,1,0:T(8,128)(2,1)S(1)} all-to-all(bf16[8,16,512]{2,1,0:T(8,128)(2,1)S(1)} %get-tuple-element.96), channel_id=1, replica_groups={{0,16,32,48,64,80,96,112},{128,144,160,176,192,208,224,240},{256,272,28..., dimensions={0} | all-to-all | bytes 262144 | tf_op jit(solution)/shard_map/all_to_all | solution.py:406
  128.4 0.4 solve.5
  128.9 33.1 %all-gather.3 = bf16[768,512]{1,0:T(8,128)(2,1)S(1)} all-gather(bf16[48,512]{1,0:T(8,128)(2,1)S(1)} %solve.5), channel_id=5, replica_groups=mesh['leaf'=32,'blk'=16] {'blk'}, dimensions={0}, use_global_device_ids=true | all-gather | bytes 835584 | tf_op jit(solution)/shard_map/all_gather | solution.py:427
  161.9 1.1 lift.1
  (27 shorter events, 0.5 us)
Async XLA Ops:
  6.5 75.5 %copy-start.3 = (bf16[256,256]{1,0:T(8,128)(2,1)S(1)}, bf16[256,256]{1,0:T(8,128)(2,1)}, u32[]{:S(2)}) copy-start(bf16[256,256]{1,0:T(8,128)(2,1)} %iterate_ref.3) | copy-start | bytes 393220
  6.5 75.5 %copy-start.4 = (f32[256,256]{1,0:T(8,128)S(1)}, f32[256,256]{1,0:T(8,128)}, u32[]{:S(2)}) copy-start(f32[256,256]{1,0:T(8,128)} %right_ref.1) | copy-start | bytes 786436
  6.5 100.9 %all-gather.6.cloned.1.call-start = ((), (), s32[]{:S(2)}) async-start(), calls=%async_computation.8 | async-start | bytes 3342336 | tf_op jit(solution)/shard_map/all_gather | solution.py:296
  6.5 98.2 %copy-start.14 = (s32[3,1,512]{2,1,0:T(1,128)S(1)}, s32[3,1,512]{2,1,0:T(1,128)}, u32[]{:S(2)}) copy-start(s32[3,1,512]{2,1,0:T(1,128)} %skeleton_ref) | copy-start | bytes 18436
  9.2 0.7 copy-start.7
  9.9 97.1 %copy-start = (bf16[3,1,512,512]{3,2,1,0:T(8,128)(2,1)S(1)}, bf16[3,1,512,512]{3,2,1,0:T(8,128)(2,1)}, u32[]{:S(2)}) copy-start(bf16[3,1,512,512]{3,2,1,0:T(8,128)(2,1)} %refs_2_.7) | copy-start | bytes 4718596
  9.9 97.1 %copy-start.1 = (bf16[3,1,512,512]{3,2,1,0:T(8,128)(2,1)S(1)}, bf16[3,1,512,512]{3,2,1,0:T(8,128)(2,1)}, u32[]{:S(2)}) copy-start(bf16[3,1,512,512]{3,2,1,0:T(8,128)(2,1)} %refs_3_.5) | copy-start | bytes 4718596
  9.9 1.1 copy-start.2
  11.0 0.7 copy-start.9
  11.7 0.7 copy-start.10
  82.1 0.9 copy-start.8
  83.3 24.1 %copy-start.5 = (f32[256,256]{1,0:T(8,128)}, f32[256,256]{1,0:T(8,128)S(1)}, u32[]{:S(2)}) copy-start(f32[256,256]{1,0:T(8,128)S(1)} %get-tuple-element.82.field_ref) | copy-start | bytes 786436
  114.7 1.9 %copy-start.11 = (bf16[3072,512]{1,0:T(8,128)(2,1)S(1)}, bf16[3072,512]{1,0:T(8,128)(2,1)}, u32[]{:S(2)}) copy-start(bf16[3072,512]{1,0:T(8,128)(2,1)} %all-gather.6.cloned.1.call-done) | copy-start | bytes 9437188
  128.4 33.5 %copy-start.6 = (f32[256,256]{1,0:T(8,128)S(1)}, f32[256,256]{1,0:T(8,128)}, u32[]{:S(2)}) copy-start(f32[256,256]{1,0:T(8,128)} %copy-done.5) | copy-start | bytes 786436
  128.4 33.5 %copy-start.12 = (bf16[3,256,512]{2,1,0:T(8,128)(2,1)S(1)}, bf16[3,256,512]{2,1,0:T(8,128)(2,1)}, u32[]{:S(2)}) copy-start(bf16[3,256,512]{2,1,0:T(8,128)(2,1)} %lift_ref.1) | copy-start | bytes 2359300
Sparse Core Ops, SparseCore 0:
  10.0 95.0 all-gather.5

commit v5 on v4

--- a/solution.py
+++ b/solution.py
@@ -9,7 +9,7 @@
 
 LEVELS = 3
 CELL = 8
-CHUNK = 1024
+CHUNK = 2048
 ROOM = 64
 KERNEL_BYTES = 16 << 20
 
@@ -27,6 +27,7 @@
 PARAMS = pltpu.CompilerParams(vmem_limit_bytes=KERNEL_BYTES)
 VMEM = pl.BlockSpec(memory_space=pltpu.VMEM)
 SMEM = pl.BlockSpec(memory_space=pltpu.SMEM)
+ANY = pl.BlockSpec(memory_space=pl.ANY)
 
 
 def dot_nt(left, right):
@@ -48,7 +49,17 @@
     return high, mid, (rest - mid).astype(BF16).astype(F32)
 
 
-def pack_kernel(points_ref, iterate_ref, mask_ref, out_ref, extra_ref):
+def pack_kernel(*refs):
+    sources, out_ref, extra_ref = refs[:3], refs[3], refs[4]
+    points_ref, iterate_ref, mask_ref = refs[5:8]
+    copies = [
+        pltpu.make_async_copy(source, target, refs[8].at[spot])
+        for spot, (source, target) in enumerate(zip(sources, refs[5:8]))
+    ]
+    for copy in copies:
+        copy.start()
+    for copy in copies:
+        copy.wait()
     count, rows, pts = out_ref.shape
     block = rows - EXTRA
     point = points_ref[...]
@@ -65,7 +76,9 @@
         out_ref[dest, block:rows, :] = extra
 
 
-def near_kernel(cell_ref, recv_ref, out_ref, acc_ref, left_ref):
+def near_kernel(cell_ref, recv_ref, inverse_ref, out_ref, kept_ref, acc_ref, left_ref, sem_ref):
+    fetch = pltpu.make_async_copy(inverse_ref, kept_ref, sem_ref)
+    fetch.start()
     count, rows, pts = recv_ref.shape
     block = rows - EXTRA
     first = cell_ref[0]
@@ -116,6 +129,7 @@
     lax.fori_loop(0, count, step, 0, unroll=2)
     for member in range(CELL):
         out_ref[member] = acc_ref[:, member * pts : (member + 1) * pts].astype(BF16)
+    fetch.wait()
 
 
 def send_field(field, out_ref):
@@ -297,25 +311,35 @@
     packed = pl.pallas_call(
         pack_kernel,
         out_shape=jax.ShapeDtypeStruct((blk_count, block + EXTRA, pts), BF16),
-        in_specs=[VMEM] * 3,
+        in_specs=[ANY] * 3,
         out_specs=VMEM,
-        scratch_shapes=[pltpu.VMEM((EXTRA, pts), F32)],
+        scratch_shapes=[
+            pltpu.VMEM((EXTRA, pts), F32),
+            pltpu.VMEM(points.shape, points.dtype),
+            pltpu.VMEM(iterate.shape, iterate.dtype),
+            pltpu.VMEM(near_mask.shape, near_mask.dtype),
+            pltpu.SemaphoreType.DMA((3,)),
+        ],
         compiler_params=PARAMS,
         name="pack",
     )(points, iterate, near_mask)
     packed = lax.all_to_all(packed, "blk", 0, 0)
-    near = pl.pallas_call(
+    near, inverse = pl.pallas_call(
         near_kernel,
-        out_shape=jax.ShapeDtypeStruct((CELL, block, pts), BF16),
-        in_specs=[SMEM, VMEM],
-        out_specs=VMEM,
+        out_shape=(
+            jax.ShapeDtypeStruct((CELL, block, pts), BF16),
+            jax.ShapeDtypeStruct(leaf_inverse.shape, leaf_inverse.dtype),
+        ),
+        in_specs=[SMEM, VMEM, ANY],
+        out_specs=(VMEM, VMEM),
         scratch_shapes=[
             pltpu.VMEM((block, CELL * pts), F32),
             pltpu.VMEM((5 * EXTRA + CELL, CELL * pts), BF16),
+            pltpu.SemaphoreType.DMA,
         ],
         compiler_params=PARAMS,
         name="near",
-    )(first, packed)
+    )(first, packed, leaf_inverse)
     near = lax.all_to_all(near, "blk", 0, 0, axis_index_groups=cells)
     field_shape = jax.ShapeDtypeStruct((pts, cols), F32)
     send_shape = jax.ShapeDtypeStruct((blk_count, share, pts), BF16)
@@ -326,7 +350,7 @@
         out_specs=(VMEM, VMEM),
         compiler_params=PARAMS,
         name="leaf",
-    )(near, right_side, iterate, leaf_inverse)
+    )(near, right_side, iterate, inverse)
 
     sent = lax.all_to_all(sent, "blk", 0, 0)
     sent, over = lax.optimization_barrier((sent, over))

time: 170 us -> 168 us (0.988)
  Pallas kernels: 20.4 us -> 18.3 us
    pallas_call x1, Pallas kernels: 11.5 us -> 9.28 us  [on_device(): pl.pallas_call(near_kernel, out_shape=(jax.ShapeDtypeStruct((CELL, block,...]
  transfers between devices with their start and end apart: 1 -> 1, of which waited for: 0 -> 0; matrix products, arithmetic and copies ran while one was open for 0% -> 0% of each run, Pallas kernels for 7% -> 6%
where the time goes in v5:
time: 168 us; the launch traced here: 167 us
  blocking collectives  129 us (77%)
  Pallas kernels  18.3 us (11%)
  between operations  14.2 us (8%)
  local copies, waits for them, and re-layouts  5.48 us (3%)
    all_to_all x1, blocking collectives, on_device(): packed = lax.all_to_all(packed, 'blk', 0, 0)  39.5 us
    all_gather x1, blocking collectives, on_device(): answer = lax.all_gather(answers[-1], 'blk', axis=0)  33 us
    all_to_all x1, blocking collectives, on_device(): sent = lax.all_to_all(sent, 'blk', 0, 0)  20.2 us
    all_to_all x1, blocking collectives, on_device(): near = lax.all_to_all(near, 'blk', 0, 0, axis_index_groups=cells)  19 us
    all_to_all x1, blocking collectives, on_device(): nodes = lax.all_to_all(nodes, 'leaf', 0, 0, axis_index_groups=groups)  10.6 us
    pallas_call x1, Pallas kernels, on_device(): pl.pallas_call(near_kernel, out_shape=(jax.ShapeDtypeStruct((CELL, block,...  9.28 us
    all_gather x2, blocking collectives, on_device(): nodes = lax.all_gather(nodes, 'leaf', axis=0, axis_index_groups=groups)  7.06 us
    unnamed x28, local copies, waits for them, and re-layouts  5.48 us
  transfers between devices with their start and end apart: 1, of which 0 were waited for; matrix products, arithmetic and copies ran while one was open for 0% of the time, Pallas kernels for 6%

profile of v5, /device:TPU:6, one launch (start us, length us, event | category | flops | bytes accessed | tf_op | source)
XLA Modules:
  0.0 167.4 jit_solution(1355288088951850269)
XLA Ops:
  6.5 2.7 %plan.1 = (bf16[192,512]{1,0:T(8,128)(2,1)S(1)}, s32[2,1,512]{2,1,0:T(1,128)S(1)}, s32[1]{0:T(128)}) custom-call(s32[1]{0:T(128)} %bitcast.2.refs_0_, s32[3,1,512]{2,1,0:T(1,128)} %skeleton_ref, bf16[3,256,512]{2,1,0:T(8,128)(2,1)} %lift_ref.1), custom_call_target="tpu_custom_call" | custom-call | tf_op jit(solution)/shard_map/plan/pallas_call | solution.py:298
  9.2 0.7 copy-done.7
  9.9 1.0 copy-done.2
  11.0 0.7 copy-done.9
  11.7 0.7 copy-done.10
  12.6 39.5 %all_to_all.40.recv_ref = bf16[16,40,256]{2,1,0:T(8,128)(2,1)S(1)} all-to-all(bf16[16,40,256]{2,1,0:T(8,128)(2,1)S(1)} %pack.1), channel_id=1, replica_groups=mesh['leaf'=32,'blk'=16] {'blk'}, dimensions={0} | all-to-all | bytes 655360 | tf_op jit(solution)/shard_map/all_to_all | solution.py:326
  52.1 0.9 copy-done.8
  53.0 9.3 %near.1 = (bf16[8,32,256]{2,1,0:T(8,128)(2,1)S(1)}, bf16[1,256,256]{2,1,0:T(8,128)(2,1)S(1)}) custom-call(s32[1]{0:T(128)} %bitcast.1.cell_ref, bf16[16,40,256]{2,1,0:T(8,128)(2,1)S(1)} %all_to_all.40.recv_ref, bf16[1,256,256]{2,1,0:T(8,128)(2,1)S(1)} %copy-done.8), custom_call_target="tpu_custom_call" | custom-call | tf_op jit(solution)/shard_map/near/pallas_call | solution.py:327
  62.3 19.0 %all_to_all.41.near_ref = bf16[8,32,256]{2,1,0:T(8,128)(2,1)S(1)} all-to-all(bf16[8,32,256]{2,1,0:T(8,128)(2,1)S(1)} %get-tuple-element.84), channel_id=1, replica_groups={{0,1,2,3,4,5,6,7},{8,9,10,11,12,13,14,15},{16,17,18,19,20,21,22,23},{24..., dimensions={0} | all-to-all | bytes 262144 | tf_op jit(solution)/shard_map/all_to_all | solution.py:343
  81.6 20.2 %all_to_all.42.recv_ref = bf16[16,16,256]{2,1,0:T(8,128)(2,1)S(1)} all-to-all(bf16[16,16,256]{2,1,0:T(8,128)(2,1)S(1)} %get-tuple-element.88), channel_id=1, replica_groups=mesh['leaf'=32,'blk'=16] {'blk'}, dimensions={0} | all-to-all | bytes 262144 | tf_op jit(solution)/shard_map/all_to_all | solution.py:355
  102.6 0.4 pick.1
  103.0 1.8 %all-gather = bf16[32,512]{1,0:T(8,128)(2,1)S(1)} all-gather(bf16[16,512]{1,0:T(8,128)(2,1)S(1)} %get-tuple-element.96), channel_id=2, replica_groups={{0,16},{32,48},{64,80},{96,112},{128,144},{160,176},{192,208},{224,240}..., dimensions={0}, use_global_device_ids=true | all-gather | bytes 49152 | tf_op jit(solution)/shard_map/all_gather | solution.py:432
  104.8 0.4 solve.3.refs_4_
  105.2 2.0 %conditional.2 = (bf16[16,512]{1,0:T(8,128)(2,1)S(1)}) conditional(s32[]{:T(128)} %bitcast.3, (bf16[16,512]{1,0:T(8,128)(2,1)S(1)}, s32[2,1,512]{2,1,0:T(1,128)S(1)}, bf16[16,512]{1,0:T(8,128)(2,1)S(1)}, bf16[16,192,512]{2,1,0:T(8,128)(2,1)}) %tuple.31, (bf16[16,512]{1,0:T(8,128)(2,1)S(1)}, bf16[3,256,512]{2,1,0:T(8,128)(2,1)}, ...), branch_computations={%region_0.1_spmd, %region_1.2_spmd} | conditional | bytes 786440 | solution.py:423
  105.2 2.0 %fast.2 = bf16[16,512]{1,0:T(8,128)(2,1)S(1)} custom-call(bf16[16,512]{1,0:T(8,128)(2,1)S(1)} %get-tuple-element.46.refs_0_, s32[2,1,512]{2,1,0:T(1,128)S(1)} %get-tuple-element.48.refs_1_, bf16[16,512]{1,0:T(8,128)(2,1)S(1)} %get-tuple-element.49.refs_2_, bf16[16,192,512]{2,1,0:T(8,128)(2,1)} %get-tuple-element.50.refs_3_), custom_call_target="tpu_custom_call" | custom-call | tf_op jit(solution)/shard_map/cond/branch_0_fun/fast/pallas_call | solution.py:369
  107.2 5.2 %all-gather.2 = bf16[64,512]{1,0:T(8,128)(2,1)S(1)} all-gather(bf16[16,512]{1,0:T(8,128)(2,1)S(1)} %get-tuple-element.99), channel_id=4, replica_groups={{0,16,32,48},{64,80,96,112},{128,144,160,176},{192,208,224,240},{256,27..., dimensions={0}, use_global_device_ids=true | all-gather | bytes 81920 | tf_op jit(solution)/shard_map/all_gather | solution.py:432
  112.5 0.4 solve.4.refs_5_
  112.9 1.5 copy-done.11
  114.3 1.0 conditional.3
  114.3 1.0 fast.3
  115.4 10.6 %all_to_all.43.refs_1_ = bf16[8,16,512]{2,1,0:T(8,128)(2,1)S(1)} all-to-all(bf16[8,16,512]{2,1,0:T(8,128)(2,1)S(1)} %get-tuple-element.100), channel_id=1, replica_groups={{0,16,32,48,64,80,96,112},{128,144,160,176,192,208,224,240},{256,272,28..., dimensions={0} | all-to-all | bytes 262144 | tf_op jit(solution)/shard_map/all_to_all | solution.py:430
  126.0 0.4 solve.5
  126.4 33.0 %all-gather.3 = bf16[768,512]{1,0:T(8,128)(2,1)S(1)} all-gather(bf16[48,512]{1,0:T(8,128)(2,1)S(1)} %solve.5), channel_id=5, replica_groups=mesh['leaf'=32,'blk'=16] {'blk'}, dimensions={0}, use_global_device_ids=true | all-gather | bytes 835584 | tf_op jit(solution)/shard_map/all_gather | solution.py:451
  159.4 1.1 lift.1
  (27 shorter events, 0.7 us)
Async XLA Ops:
  6.5 74.7 %copy-start.3 = (bf16[256,256]{1,0:T(8,128)(2,1)S(1)}, bf16[256,256]{1,0:T(8,128)(2,1)}, u32[]{:S(2)}) copy-start(bf16[256,256]{1,0:T(8,128)(2,1)} %iterate_ref.1) | copy-start | bytes 393220
  6.5 74.7 %copy-start.4 = (f32[256,256]{1,0:T(8,128)S(1)}, f32[256,256]{1,0:T(8,128)}, u32[]{:S(2)}) copy-start(f32[256,256]{1,0:T(8,128)} %right_ref.1) | copy-start | bytes 786436
  6.5 98.7 %all-gather.6.cloned.1.call-start = ((), (), s32[]{:S(2)}) async-start(), calls=%async_computation.8 | async-start | bytes 3342336 | tf_op jit(solution)/shard_map/all_gather | solution.py:310
  6.5 96.0 %copy-start.14 = (s32[3,1,512]{2,1,0:T(1,128)S(1)}, s32[3,1,512]{2,1,0:T(1,128)}, u32[]{:S(2)}) copy-start(s32[3,1,512]{2,1,0:T(1,128)} %skeleton_ref) | copy-start | bytes 18436
  9.2 0.7 copy-start.7
  9.9 94.9 %copy-start = (bf16[3,1,512,512]{3,2,1,0:T(8,128)(2,1)S(1)}, bf16[3,1,512,512]{3,2,1,0:T(8,128)(2,1)}, u32[]{:S(2)}) copy-start(bf16[3,1,512,512]{3,2,1,0:T(8,128)(2,1)} %refs_2_.9) | copy-start | bytes 4718596
  9.9 94.9 %copy-start.1 = (bf16[3,1,512,512]{3,2,1,0:T(8,128)(2,1)S(1)}, bf16[3,1,512,512]{3,2,1,0:T(8,128)(2,1)}, u32[]{:S(2)}) copy-start(bf16[3,1,512,512]{3,2,1,0:T(8,128)(2,1)} %refs_3_.5) | copy-start | bytes 4718596
  9.9 1.1 copy-start.2
  11.0 0.7 copy-start.9
  11.7 0.7 copy-start.10
  52.1 0.9 copy-start.8
  81.6 23.6 %copy-start.5 = (f32[256,256]{1,0:T(8,128)}, f32[256,256]{1,0:T(8,128)S(1)}, u32[]{:S(2)}) copy-start(f32[256,256]{1,0:T(8,128)S(1)} %get-tuple-element.86.field_ref) | copy-start | bytes 786436
  112.5 1.9 %copy-start.11 = (bf16[3072,512]{1,0:T(8,128)(2,1)S(1)}, bf16[3072,512]{1,0:T(8,128)(2,1)}, u32[]{:S(2)}) copy-start(bf16[3072,512]{1,0:T(8,128)(2,1)} %all-gather.6.cloned.1.call-done) | copy-start | bytes 9437188
  126.0 33.4 %copy-start.6 = (f32[256,256]{1,0:T(8,128)S(1)}, f32[256,256]{1,0:T(8,128)}, u32[]{:S(2)}) copy-start(f32[256,256]{1,0:T(8,128)} %copy-done.5) | copy-start | bytes 786436
  126.0 33.4 %copy-start.12 = (bf16[3,256,512]{2,1,0:T(8,128)(2,1)S(1)}, bf16[3,256,512]{2,1,0:T(8,128)(2,1)}, u32[]{:S(2)}) copy-start(bf16[3,256,512]{2,1,0:T(8,128)(2,1)} %lift_ref.1) | copy-start | bytes 2359300
Sparse Core Ops, SparseCore 0:
  10.0 94.4 all-gather.5
